TPU v7x, 128 devices: a whole 4x4x4 slice. The times are simulated.
128 devices in a mesh: dom: 16 (over y_hi, x, core), feat: 8 (over z, y_lo).
Axes of the slice: x: 4, y: 4 (y_hi: 2, y_lo: 2; y = y_hi * 2 + y_lo), z: 4, core: 2. Of those that a mesh axis runs over, the one named last changes fastest.
Arguments:
- state: bfloat16 [512, 32768], P('feat', 'dom'), may hold values from -3 to 3
- inputs: bfloat16 [2, 32768], P(None, 'dom'), may hold values from -6 to 6
- adj_tiles: bfloat16 [256, 4, 128, 128], P('dom'), may hold values from -0.25 to 0.25
- adj_cols: int32 [256, 4], P('dom'), may hold values from 0 to 17, as said below
- valid_rows: int32 [16], P('dom'), may hold values from 1024 to 2048, as said below
- cluster_of: int32 [32768], P('dom'), may hold values from 0 to 4095
- w_gates: bfloat16 [3, 512, 4, 512], P(None, 'feat'), may hold values from -0.125 to 0.125
- w_input: bfloat16 [3, 512, 2], P(None, 'feat'), may hold values from -4 to 4
- bias: float32 [3, 512], P(None, 'feat'), may hold values from -4 to 4
- w_value: bfloat16 [8, 64, 64], P('feat'), may hold values from -0.75 to 0.75
- source_emb: float32 [8, 10, 4096], P('feat'), may hold values from -5 to 5
- target_emb: float32 [8, 10, 4096], P('feat'), may hold values from -5 to 5
- coarse_tiles: bfloat16 [32, 2, 128, 128], replicated, may hold values from -0.375 to 0.375
- coarse_cols: int32 [32, 2], replicated, may hold values from 0 to 31
Outputs:
- new_state: bfloat16 [512, 32768], P('feat', 'dom')
Inputs may be any that keep to these rules, and one draw needn't show every extreme that they name: `adj_cols`: for local row tile t of a partition (t counted from 0 in the partition), every entry lies in t to t + 2, the first is t and the last is t + 2. `valid_rows`: some partition has all 2048 rows valid and another exactly half of them.
All inputs are finite; a program needn't handle non-finite values.
Results may differ from a plain program's by a relative error of at most 0.003.
Values may be sent and summed in bfloat16 or wider, within the bound.
A program may use at most 64 MiB of HBM per device.

v0:
```python
import math

import jax
import jax.numpy as jnp
from jax import lax
from jax.sharding import PartitionSpec as P


def extended_2(array, sides, width):
    for axis, dim in sides:
        peers, length = (lax.axis_size(axis), array.shape[dim])
        up = [(i, (i + 1) % peers) for i in range(peers)]
        down = [(j, i) for i, j in up]
        last = lax.slice_in_dim(array, length - width, length, axis=dim)
        leading = lax.slice_in_dim(array, 0, width, axis=dim)
        before = lax.ppermute(last, axis, up)
        after = lax.ppermute(leading, axis, down)
        array = jnp.concatenate([before, array, after], axis=dim)
    return array


def diffuse(states, adj_tiles, adj_cols, row_mask):
    tile_size = adj_tiles.shape[2]
    channels, row_count = states.shape
    extended = extended_2(states, (("dom", 1),), tile_size)
    extended = extended.reshape(channels, row_count // tile_size + 2, tile_size)
    picked = extended[:, adj_cols]
    result = jnp.einsum("hnkj,nkji->hni", picked, adj_tiles, preferred_element_type=jnp.float32)
    return (result.reshape(channels, row_count) * row_mask).astype(jnp.bfloat16)


def project(pooled, w_value):
    heads_here, head_size = (w_value.shape[0], w_value.shape[1])
    grouped = pooled.reshape(heads_here, head_size, pooled.shape[1])
    return jnp.einsum(
        "hde,hec->hdc", w_value.astype(jnp.float32), grouped, precision=lax.Precision.HIGHEST
    ).astype(jnp.bfloat16)


def attend(source_cols, target_emb, values):
    heads_here, emb_dim, query_count = source_cols.shape
    block_rows = math.gcd(query_count, 512)
    blocks = source_cols.reshape(heads_here, emb_dim, query_count // block_rows, block_rows)
    blocks = jnp.moveaxis(blocks, 2, 0)

    def one_block(source_block):
        scores = jnp.einsum(
            "hei,hej->hij", source_block, target_emb, precision=lax.Precision.HIGHEST
        )
        scores = jnp.maximum(scores, 0.0)
        row_peak = jnp.max(scores, axis=2, keepdims=True)
        raised = jnp.exp(scores - row_peak)
        weights = (raised / jnp.sum(raised, axis=2, keepdims=True)).astype(jnp.bfloat16)
        return jnp.einsum("hdj,hij->hdi", values, weights, preferred_element_type=jnp.float32)

    outputs = lax.map(one_block, blocks)
    outputs = jnp.moveaxis(outputs, 0, 2)
    return outputs.reshape(heads_here, values.shape[1], query_count)


def body(
    state,
    inputs,
    adj_tiles,
    adj_cols,
    valid_rows,
    cluster_of,
    w_gates,
    w_input,
    bias,
    w_value,
    source_emb,
    target_emb,
    coarse_tiles,
    coarse_cols,
):
    channels, row_count = state.shape
    cluster_count = source_emb.shape[2]
    row_mask = (jnp.arange(row_count, dtype=jnp.int32) < valid_rows[0]).astype(jnp.float32)
    masked = (state.astype(jnp.float32) * row_mask).astype(jnp.bfloat16)
    hop_one = diffuse(masked, adj_tiles, adj_cols, row_mask)
    hop_two = diffuse(hop_one, adj_tiles, adj_cols, row_mask)
    member = (cluster_of[:, None] == jnp.arange(cluster_count, dtype=jnp.int32)[None, :]).astype(
        jnp.bfloat16
    )
    cluster_sums = jnp.dot(masked, member, preferred_element_type=jnp.float32)
    counts = jnp.dot(
        row_mask.astype(jnp.bfloat16)[None, :], member, preferred_element_type=jnp.float32
    )
    cluster_sums, counts = (
        lax.psum(cluster_sums.astype(jnp.bfloat16), "dom").astype(jnp.float32),
        lax.psum(counts.astype(jnp.bfloat16), "dom").astype(jnp.float32),
    )
    pooled = cluster_sums / jnp.maximum(counts, 1.0)
    all_values = project(pooled, w_value)
    attended = attend(source_emb, target_emb, all_values)
    coarse_attn = (pooled + attended.reshape(channels, cluster_count)).astype(jnp.bfloat16)
    tile_size = coarse_tiles.shape[2]
    coarse_grid = coarse_attn.reshape(channels, cluster_count // tile_size, tile_size)
    picked = coarse_grid[:, coarse_cols]
    coarse_terms = jnp.einsum(
        "hnkj,nkji->hni", picked, coarse_tiles, preferred_element_type=jnp.float32
    )
    coarse = (
        coarse_attn.astype(jnp.float32) + coarse_terms.reshape(channels, cluster_count)
    ).astype(jnp.bfloat16)
    unpooled = jnp.take(coarse, cluster_of, axis=1)
    features = jnp.stack([masked, hop_one, hop_two, unpooled])
    gate_sums = jnp.einsum(
        "ghkc,kcr->ghr",
        w_gates,
        lax.all_gather(features, "feat", axis=1, tiled=True),
        preferred_element_type=jnp.float32,
    )
    input_terms = (
        jnp.einsum("ghf,fr->ghr", w_input, inputs, preferred_element_type=jnp.float32)
        + bias[:, :, None]
    )
    update = jax.nn.sigmoid(input_terms[0] + gate_sums[0])
    reset = jax.nn.sigmoid(input_terms[1] + gate_sums[1])
    candidate = jnp.tanh(input_terms[2] + reset * gate_sums[2])
    fresh_state = (update * masked.astype(jnp.float32) + (1.0 - update) * candidate) * row_mask
    return fresh_state.astype(jnp.bfloat16)


def solution(mesh):
    return jax.shard_map(
        body,
        mesh=mesh,
        in_specs=(
            P("feat", "dom"),
            P(None, "dom"),
            P("dom", None, None, None),
            P("dom", None),
            P("dom"),
            P("dom"),
            P(None, "feat", None, None),
            P(None, "feat", None),
            P(None, "feat"),
            P("feat", None, None),
            P("feat", None, None),
            P("feat", None, None),
            P(),
            P(),
        ),
        out_specs=P("feat", "dom"),
        check_vma=False,
    )
```

profile of v0, /device:TPU:1, one launch (start us, length us, event | category | flops | bytes accessed | tf_op | source)
XLA Modules:
  0.0 465.1 jit_solution(15305916377223197281)
XLA Ops:
  8.4 8.4 %fusion.15 = bf16[64,4096]{1,0:T(8,128)(2,1)} fusion(bf16[64,2048]{1,0:T(8,128)(2,1)S(1)} %multiply_convert_fusion.2, s32[2048]{0:T(1024)} %param.21), kind=kOutput, calls=%fused_computation.25 | convolution fusion | flops 1082392576 | bytes 794624 | tf_op jit(solution)/shard_map/dot_general | solution.py:86
  21.8 6.0 %fusion.9 = f32[1,4096]{1,0:T(1,128)S(1)} fusion(bf16[2048,1]{0,1:T(2,128)(2,1)S(1)} %reshape.241, s32[2048]{0:T(1024)S(1)} %copy-done.7), kind=kOutput, calls=%fused_computation.19 | convolution fusion | flops 25165824 | bytes 28672 | tf_op jit(solution)/shard_map/dot_general | solution.py:87
  27.9 67.7 %psum.15 = bf16[1,4096]{1,0:T(2,128)(2,1)S(1)} all-reduce(bf16[1,4096]{1,0:T(2,128)(2,1)S(1)} %convert_element_type.97), channel_id=1, replica_groups=mesh['dom'=16,'feat'=8] {'dom'}, use_global_device_ids=true, to_apply=%region_1.0 | all-reduce | flops 4096 | bytes 16384 | tf_op jit(solution)/shard_map/psum | solution.py:92
  100.3 5.9 %collective-permute-start.3 = (bf16[64,128]{1,0:T(8,128)(2,1)S(1)}, bf16[64,128]{1,0:T(8,128)(2,1)S(1)}, u32[]{:S(2)}, u32[]{:S(2)}) collective-permute-start(bf16[64,128]{1,0:T(8,128)(2,1)S(1)} %get-tuple-element.51), channel_id=1, source_target_pairs={{8,0},{16,8},{24,16},{32,24},{40,32},{48,40},{56,48},{64,56},{72,6... | collective-permute-start | bytes 49160 | tf_op jit(solution)/shard_map/ppermute | solution.py:17
  118.0 41.8 %all-reduce.2.cloned.1.call-done = bf16[64,4096]{1,0:T(8,128)(2,1)} async-done(((bf16[64,4096]{1,0:T(8,128)(2,1)}), bf16[64,4096]{1,0:T(8,128)(2,1)}) %all-reduce.2.cloned.1.call-update) | async-done | bytes 524304 | tf_op jit(solution)/shard_map/psum | solution.py:91
  162.4 100.1 %while.10 = (s32[]{:T(128)}, f32[8,1,64,512]{3,2,1,0:T(8,128)}, f32[8,1,10,512]{3,0,1,2:T(8,128)}, f32[1,10,4096]{2,0,1:T(1,128)S(1)}, bf16[1,64,4096]{2,1,0:T(8,128)(2,1)}, /*index=5*/s32[]{:T(128)}) while((s32[]{:T(128)}, f32[8,1,64,512]{3,2,1,0:T(8,128)}, f32[8,1,10,512]{3,0,1,2:T(8,128)}, f32[1,10,4096]{2,0,1:T(1,128)S(1)}, ...), condition=%wide.region_5.6_spmd, body=%wide.region_2.5_spmd.sunk | while | flops 538967040 | bytes 28153968 | solution.py:56
  163.4 7.2 %maximum_reduce_fusion.2 = (f32[512]{0:T(512)S(1)}, f32[512,4096]{1,0:T(8,128)S(1)}) fusion(f32[1,10,4096]{2,0,1:T(1,128)S(1)} %get-tuple-element.108, f32[1,1,10,512]{3,0,1,2:T(1,128)S(1)} %constant_dynamic-slice_fusion.2), kind=kOutput, calls=%fused_computation.6.clone.1 | convolution fusion | flops 255852032 | bytes 8574976 | tf_op jit(solution)/shard_map/while/body/eval_jaxpr/hei,hej->hij/dot_general | solution.py:47
  172.1 2.9 fusion.65
  175.9 7.2 %maximum_reduce_fusion.2 = (f32[512]{0:T(512)S(1)}, f32[512,4096]{1,0:T(8,128)S(1)}) fusion(f32[1,10,4096]{2,0,1:T(1,128)S(1)} %get-tuple-element.108, f32[1,1,10,512]{3,0,1,2:T(1,128)S(1)} %constant_dynamic-slice_fusion.2), kind=kOutput, calls=%fused_computation.6.clone.1 | convolution fusion | flops 255852032 | bytes 8574976 | tf_op jit(solution)/shard_map/while/body/eval_jaxpr/hei,hej->hij/dot_general | solution.py:47
  184.6 2.9 fusion.65
  188.4 7.2 %maximum_reduce_fusion.2 = (f32[512]{0:T(512)S(1)}, f32[512,4096]{1,0:T(8,128)S(1)}) fusion(f32[1,10,4096]{2,0,1:T(1,128)S(1)} %get-tuple-element.108, f32[1,1,10,512]{3,0,1,2:T(1,128)S(1)} %constant_dynamic-slice_fusion.2), kind=kOutput, calls=%fused_computation.6.clone.1 | convolution fusion | flops 255852032 | bytes 8574976 | tf_op jit(solution)/shard_map/while/body/eval_jaxpr/hei,hej->hij/dot_general | solution.py:47
  197.1 2.9 fusion.65
  200.9 7.2 %maximum_reduce_fusion.2 = (f32[512]{0:T(512)S(1)}, f32[512,4096]{1,0:T(8,128)S(1)}) fusion(f32[1,10,4096]{2,0,1:T(1,128)S(1)} %get-tuple-element.108, f32[1,1,10,512]{3,0,1,2:T(1,128)S(1)} %constant_dynamic-slice_fusion.2), kind=kOutput, calls=%fused_computation.6.clone.1 | convolution fusion | flops 255852032 | bytes 8574976 | tf_op jit(solution)/shard_map/while/body/eval_jaxpr/hei,hej->hij/dot_general | solution.py:47
  209.6 2.9 fusion.65
  213.4 7.2 %maximum_reduce_fusion.2 = (f32[512]{0:T(512)S(1)}, f32[512,4096]{1,0:T(8,128)S(1)}) fusion(f32[1,10,4096]{2,0,1:T(1,128)S(1)} %get-tuple-element.108, f32[1,1,10,512]{3,0,1,2:T(1,128)S(1)} %constant_dynamic-slice_fusion.2), kind=kOutput, calls=%fused_computation.6.clone.1 | convolution fusion | flops 255852032 | bytes 8574976 | tf_op jit(solution)/shard_map/while/body/eval_jaxpr/hei,hej->hij/dot_general | solution.py:47
  225.9 7.2 %maximum_reduce_fusion.2 = (f32[512]{0:T(512)S(1)}, f32[512,4096]{1,0:T(8,128)S(1)}) fusion(f32[1,10,4096]{2,0,1:T(1,128)S(1)} %get-tuple-element.108, f32[1,1,10,512]{3,0,1,2:T(1,128)S(1)} %constant_dynamic-slice_fusion.2), kind=kOutput, calls=%fused_computation.6.clone.1 | convolution fusion | flops 255852032 | bytes 8574976 | tf_op jit(solution)/shard_map/while/body/eval_jaxpr/hei,hej->hij/dot_general | solution.py:47
  234.6 2.9 fusion.65
  238.4 7.2 %maximum_reduce_fusion.2 = (f32[512]{0:T(512)S(1)}, f32[512,4096]{1,0:T(8,128)S(1)}) fusion(f32[1,10,4096]{2,0,1:T(1,128)S(1)} %get-tuple-element.108, f32[1,1,10,512]{3,0,1,2:T(1,128)S(1)} %constant_dynamic-slice_fusion.2), kind=kOutput, calls=%fused_computation.6.clone.1 | convolution fusion | flops 255852032 | bytes 8574976 | tf_op jit(solution)/shard_map/while/body/eval_jaxpr/hei,hej->hij/dot_general | solution.py:47
  247.1 2.9 fusion.65
  250.9 7.2 %maximum_reduce_fusion.2 = (f32[512]{0:T(512)S(1)}, f32[512,4096]{1,0:T(8,128)S(1)}) fusion(f32[1,10,4096]{2,0,1:T(1,128)S(1)} %get-tuple-element.108, f32[1,1,10,512]{3,0,1,2:T(1,128)S(1)} %constant_dynamic-slice_fusion.2), kind=kOutput, calls=%fused_computation.6.clone.1 | convolution fusion | flops 255852032 | bytes 8574976 | tf_op jit(solution)/shard_map/while/body/eval_jaxpr/hei,hej->hij/dot_general | solution.py:47
  259.6 2.9 fusion.65
  270.6 8.0 %gather_fusion.3 = bf16[2048,64]{1,0:T(8,128)(2,1)} fusion(bf16[64,4096]{0,1:T(8,128)(2,1)S(1)} %copy.39, s32[2048]{0:T(1024)S(1)} %fusion.43), kind=kCustom, calls=%fused_computation.3 | custom fusion | bytes 532480 | tf_op jit(solution)/shard_map/jit(_take)/gather | solution.py:107
  283.8 167.9 %all-gather.2.cloned.1.call-done = bf16[4,512,2048]{2,1,0:T(8,128)(2,1)} async-done(((bf16[4,64,2048]{2,1,0:T(8,128)(2,1)}), bf16[4,512,2048]{2,1,0:T(8,128)(2,1)}) %all-gather.2.cloned.1.call-update) | async-done | bytes 8388624 | tf_op jit(solution)/shard_map/all_gather | solution.py:112
  451.7 5.4 %fusion.17 = f32[3,64,2048]{2,1,0:T(8,128)S(1)} fusion(bf16[4,512,2048]{2,1,0:T(8,128)(2,1)} %all-gather.2.cloned.1.call-done, bf16[3,64,4,512]{3,2,1,0:T(4,128)(2,1)} %param.22), kind=kOutput, calls=%fused_computation.28 | convolution fusion | flops 1610612736 | bytes 10747904 | tf_op jit(solution)/shard_map/ghkc,kcr->ghr/dot_general | solution.py:109
  (120 shorter events, 61.7 us)
Async XLA Ops:
  6.5 91.3 %copy-start = (bf16[16,4,128,128]{3,2,1,0:T(8,128)(2,1)S(1)}, bf16[16,4,128,128]{3,2,1,0:T(8,128)(2,1)}, u32[]{:S(2)}) copy-start(bf16[16,4,128,128]{3,2,1,0:T(8,128)(2,1)} %param.18) | copy-start | bytes 6291460
  6.5 13.3 %copy-start.3 = (bf16[64,2048]{1,0:T(8,128)(2,1)S(1)}, bf16[64,2048]{1,0:T(8,128)(2,1)}, u32[]{:S(2)}) copy-start(bf16[64,2048]{1,0:T(8,128)(2,1)} %param.16) | copy-start | bytes 786436
  6.5 13.3 %copy-start.7 = (s32[2048]{0:T(1024)S(1)}, s32[2048]{0:T(1024)}, u32[]{:S(2)}) copy-start(s32[2048]{0:T(1024)} %param.21) | copy-start | bytes 24580
  6.5 14.0 %copy-start.6 = (f32[1,10,4096]{2,0,1:T(1,128)S(1)}, f32[1,10,4096]{2,0,1:T(1,128)}, u32[]{:S(2)}) copy-start(f32[1,10,4096]{2,0,1:T(1,128)} %param.26) | copy-start | bytes 491524
  6.5 153.2 %all-reduce.2.cloned.1.call-start = ((), (), s32[]{:S(2)}) async-start(), calls=%async_computation | async-start | bytes 1048576 | tf_op jit(solution)/shard_map/psum | solution.py:91
  16.8 78.9 %copy-start.12 = (s32[32,2]{0,1:T(2,128)S(1)}, s32[32,2]{0,1:T(2,128)}, u32[]{:S(2)}) copy-start(s32[32,2]{0,1:T(2,128)} %param.29) | copy-start | bytes 772
  16.8 78.9 %copy-start.10 = (s32[16,4]{0,1:T(4,128)S(1)}, s32[16,4]{0,1:T(4,128)}, u32[]{:S(2)}) copy-start(s32[16,4]{0,1:T(4,128)} %param.19) | copy-start | bytes 772
  16.8 434.9 %all-gather.2.cloned.1.call-start = ((), (), s32[]{:S(2)}) async-start(), calls=%async_computation.1 | async-start | bytes 9437184 | tf_op jit(solution)/shard_map/all_gather | solution.py:112
  16.9 79.2 %collective-permute-start.1 = (bf16[64,128]{1,0:T(8,128)(2,1)S(1)}, bf16[64,128]{1,0:T(8,128)(2,1)S(1)}, u32[]{:S(2)}, u32[]{:S(2)}) collective-permute-start(bf16[64,128]{1,0:T(8,128)(2,1)S(1)} %get-tuple-element.53), channel_id=1, source_target_pairs={{8,0},{16,8},{24,16},{32,24},{40,32},{48,40},{56,48},{64,56},{72,6... | collective-permute-start | bytes 49160 | tf_op jit(solution)/shard_map/ppermute | solution.py:17
  18.3 77.7 %collective-permute-start = (bf16[64,128]{1,0:T(8,128)(2,1)S(1)}, bf16[64,128]{1,0:T(8,128)(2,1)S(1)}, u32[]{:S(2)}, u32[]{:S(2)}) collective-permute-start(bf16[64,128]{1,0:T(8,128)(2,1)S(1)} %get-tuple-element.52), channel_id=1, source_target_pairs={{0,8},{8,16},{16,24},{24,32},{32,40},{40,48},{48,56},{56,64},{64,7... | collective-permute-start | bytes 49160 | tf_op jit(solution)/shard_map/ppermute | solution.py:16
  97.8 62.0 %copy-start.13 = (bf16[1,64,64]{2,1,0:T(8,128)(2,1)S(1)}, bf16[1,64,64]{2,1,0:T(8,128)(2,1)}, u32[]{:S(2)}) copy-start(bf16[1,64,64]{2,1,0:T(8,128)(2,1)} %param.25) | copy-start | bytes 24580
  99.6 62.9 %copy-start.1 = (f32[1,10,4096]{2,0,1:T(1,128)S(1)}, f32[1,10,4096]{2,0,1:T(1,128)}, u32[]{:S(2)}) copy-start(f32[1,10,4096]{2,0,1:T(1,128)} %param.27) | copy-start | bytes 491524
  100.3 8.2 %collective-permute-start.3 = (bf16[64,128]{1,0:T(8,128)(2,1)S(1)}, bf16[64,128]{1,0:T(8,128)(2,1)S(1)}, u32[]{:S(2)}, u32[]{:S(2)}) collective-permute-start(bf16[64,128]{1,0:T(8,128)(2,1)S(1)} %get-tuple-element.51), channel_id=1, source_target_pairs={{8,0},{16,8},{24,16},{32,24},{40,32},{48,40},{56,48},{64,56},{72,6... | collective-permute-start | bytes 49160 | tf_op jit(solution)/shard_map/ppermute | solution.py:17
  106.3 2.3 collective-permute-start.2
  162.4 101.4 %copy-start.5 = (bf16[64,4096]{1,0:T(8,128)(2,1)S(1)}, bf16[64,4096]{1,0:T(8,128)(2,1)}, u32[]{:S(2)}) copy-start(bf16[64,4096]{1,0:T(8,128)(2,1)} %all-reduce.2.cloned.1.call-done) | copy-start | bytes 1572868
  163.4 8.7 %copy-start.14 = (bf16[1,64,4096]{2,1,0:T(8,128)(2,1)S(1)}, bf16[1,64,4096]{2,1,0:T(8,128)(2,1)}, u32[]{:S(2)}) copy-start(bf16[1,64,4096]{2,1,0:T(8,128)(2,1)} %get-tuple-element.109) | copy-start | bytes 1572868 | tf_op jit(solution)/shard_map/while
  175.9 8.7 %copy-start.14 = (bf16[1,64,4096]{2,1,0:T(8,128)(2,1)S(1)}, bf16[1,64,4096]{2,1,0:T(8,128)(2,1)}, u32[]{:S(2)}) copy-start(bf16[1,64,4096]{2,1,0:T(8,128)(2,1)} %get-tuple-element.109) | copy-start | bytes 1572868 | tf_op jit(solution)/shard_map/while
  188.4 8.7 %copy-start.14 = (bf16[1,64,4096]{2,1,0:T(8,128)(2,1)S(1)}, bf16[1,64,4096]{2,1,0:T(8,128)(2,1)}, u32[]{:S(2)}) copy-start(bf16[1,64,4096]{2,1,0:T(8,128)(2,1)} %get-tuple-element.109) | copy-start | bytes 1572868 | tf_op jit(solution)/shard_map/while
  213.4 8.7 %copy-start.14 = (bf16[1,64,4096]{2,1,0:T(8,128)(2,1)S(1)}, bf16[1,64,4096]{2,1,0:T(8,128)(2,1)}, u32[]{:S(2)}) copy-start(bf16[1,64,4096]{2,1,0:T(8,128)(2,1)} %get-tuple-element.109) | copy-start | bytes 1572868 | tf_op jit(solution)/shard_map/while
  238.4 8.7 %copy-start.14 = (bf16[1,64,4096]{2,1,0:T(8,128)(2,1)S(1)}, bf16[1,64,4096]{2,1,0:T(8,128)(2,1)}, u32[]{:S(2)}) copy-start(bf16[1,64,4096]{2,1,0:T(8,128)(2,1)} %get-tuple-element.109) | copy-start | bytes 1572868 | tf_op jit(solution)/shard_map/while
  250.9 8.7 %copy-start.14 = (bf16[1,64,4096]{2,1,0:T(8,128)(2,1)S(1)}, bf16[1,64,4096]{2,1,0:T(8,128)(2,1)}, u32[]{:S(2)}) copy-start(bf16[1,64,4096]{2,1,0:T(8,128)(2,1)} %get-tuple-element.109) | copy-start | bytes 1572868 | tf_op jit(solution)/shard_map/while
  264.1 18.0 %copy-start.8 = (bf16[2,2048]{1,0:T(2,128)(2,1)S(1)}, bf16[2,2048]{1,0:T(2,128)(2,1)}, u32[]{:S(2)}) copy-start(bf16[2,2048]{1,0:T(2,128)(2,1)} %param.17) | copy-start | bytes 24580
  264.1 18.0 %copy-start.9 = (f32[3,64]{1,0:T(4,128)S(1)}, f32[3,64]{1,0:T(4,128)}, u32[]{:S(2)}) copy-start(f32[3,64]{1,0:T(4,128)} %param.24) | copy-start | bytes 2308
  264.1 18.0 %copy-start.11 = (bf16[3,64,2]{1,2,0:T(2,128)(2,1)S(1)}, bf16[3,64,2]{1,2,0:T(2,128)(2,1)}, u32[]{:S(2)}) copy-start(bf16[3,64,2]{1,2,0:T(2,128)(2,1)} %param.23) | copy-start | bytes 2308
  (4 other events, 23.5 us)
Sparse Core Ops, SparseCore 0:
  16.9 142.7 all-reduce.1
  282.3 169.3 all-gather.1
where the time goes:
time: 466 us; the launch traced here: 465 us
  waiting for transfers between devices  210 us (45%)
  matrix products  110 us (24%)
  blocking collectives  67.7 us (15%)
  local copies, waits for them, and re-layouts  32 us (7%)
  other arithmetic  21.6 us (5%)
  between operations  14.5 us (3%)
  starting transfers between devices  8.94 us (2%)
    all_gather x1, waiting for transfers between devices, body(): lax.all_gather(features, 'feat', axis=1, tiled=True)  168 us
    psum x1, blocking collectives, body(): lax.psum(counts.astype(jnp.bfloat16), 'dom').astype(jnp.float32)  67.7 us
    dot_general x8, matrix products, one_block(): jnp.einsum('hei,hej->hij', source_block, target_emb, precision=lax.Precis...  57.3 us
    psum x1, waiting for transfers between devices, body(): lax.psum(cluster_sums.astype(jnp.bfloat16), 'dom').astype(jnp.float32)  41.8 us
    dot_general x8, matrix products, one_block(): jnp.einsum('hdj,hij->hdi', values, weights, preferred_element_type=jnp.fl...  23.1 us
    reduce_sum x8, other arithmetic, one_block(): jnp.sum(raised, axis=2, keepdims=True)  12 us
  transfers between devices with their start and end apart: 6, of which 2 were waited for; matrix products, arithmetic and copies ran while one was open for 5% of the time, Pallas kernels for 0%

commit v1 on v0

v1 whole, which is shorter than its diff:
```python
import jax
import jax.numpy as jnp
from jax import lax
from jax.experimental import pallas as pl
from jax.experimental.pallas import tpu as pltpu
from jax.sharding import PartitionSpec as P

MESH = pl.DeviceIdType.MESH
BF = jnp.bfloat16
F32 = jnp.float32
N_MSG = 80


def dot(a, b, dims=((1,), (0,))):
    return lax.dot_general(a, b, (dims, ((), ())), preferred_element_type=F32)


def split3(v):
    a = v.astype(BF)
    r = v - a.astype(F32)
    b = r.astype(BF)
    c = (r - b.astype(F32)).astype(BF)
    return a, b, c


def split_counts(total):
    high = jnp.floor(total * (1.0 / 256.0)) * 256.0
    low = total - high
    row = lax.broadcasted_iota(jnp.int32, (16, total.shape[1]), 0)
    return jnp.where(row == 0, high, jnp.where(row == 1, low, 0.0))


def kernel(
    state, xin, adj_hbm, adj_cols, valid, cluster, wg_hbm, w_in, bias, w_val, src, tgt,
    ct_hbm, ccols, out,
    mext, halo, ohlo, base, pl_lhs, pool, r1, s1, r2, s2, r3, t6, s6, scores, expo,
    vals, ca, gall, gmix, ubuf, vbuf, w1m, gsum, adj, wg, ct,
    ssem, rsem, lsem,
):
    d = lax.axis_index("dom")
    f = lax.axis_index("feat")
    core, x, yh = d % 2, (d // 2) % 4, d // 8
    z, yl = f // 2, f % 2
    partner = d + 1 - 2 * core
    xp, xm, x2 = (x + 1) % 4, (x + 3) % 4, (x + 2) % 4
    zp, zm, z2 = (z + 1) % 4, (z + 3) % 4, (z + 2) % 4
    fy = f + 1 - 2 * yl
    yother = (d + 8) % 16
    dleft, dright = (d + 15) % 16, (d + 1) % 16
    didx = lambda a, b, c: a * 8 + b * 2 + c
    fidx = lambda a, b: a * 2 + b
    to_dom = lambda i: (i, f)
    to_feat = lambda i: (d, i)

    msgs = []

    def send(src_ref, dst_ref, dev):
        i = len(msgs)
        cp = pltpu.make_async_remote_copy(
            src_ref=src_ref, dst_ref=dst_ref, send_sem=ssem.at[i], recv_sem=rsem.at[i],
            device_id=dev, device_id_type=MESH,
        )
        cp.start()
        msgs.append(cp)
        return cp

    loc = [
        pltpu.make_async_copy(wg_hbm, wg, lsem.at[0]),
        pltpu.make_async_copy(adj_hbm, adj, lsem.at[1]),
        pltpu.make_async_copy(ct_hbm, ct, lsem.at[2]),
    ]
    for c in loc:
        c.start()

    barrier = pltpu.get_barrier_semaphore()
    x_peers = [didx(yh, xp, core), didx(yh, xm, core), didx(yh, x2, core)]
    f_peers = [(f + k) % 8 for k in range(1, 8)]
    cross = (d + 15 + 2 * core) % 16
    dom_peers = [partner, cross, yother] + x_peers
    for p in dom_peers:
        pl.semaphore_signal(barrier, inc=1, device_id=to_dom(p), device_id_type=MESH)
    for p in f_peers:
        pl.semaphore_signal(barrier, inc=1, device_id=to_feat(p), device_id_type=MESH)

    nvalid = valid[0]
    mask = (lax.broadcasted_iota(jnp.int32, (1, 2048), 1) < nvalid).astype(F32)
    masked32 = state[...].astype(F32) * mask
    myrows = pl.ds(pl.multiple_of(f * 64, 64), 64)
    own = pl.ds(128, 2048)
    mext[myrows, own] = masked32.astype(BF)
    base[0:64, :] = masked32
    row16 = lax.broadcasted_iota(jnp.int32, (16, 2048), 0)
    base[64:80, :] = jnp.where(row16 == 0, mask, 0.0)
    low = cluster[...] & 255
    high = cluster[...] >> 8
    ohlo[...] = (lax.broadcasted_iota(jnp.int32, (256, 2048), 0) == low).astype(F32).astype(BF)

    for c in range(2):
        for xx in range(4):
            for yy in range(2):
                slot = c * 8 + xx * 2 + yy
                hit = high == (yy * 8 + xx * 2 + c)
                pl_lhs[slot * 80:(slot + 1) * 80, :] = jnp.where(hit, base[...], 0.0).astype(BF)

    for q in range(4):
        res = dot(pl_lhs[q * 320:(q + 1) * 320, :], ohlo[...], ((1,), (1,)))
        for k in range(4):
            slot = q * 4 + k
            r = res[k * 80:(k + 1) * 80]
            pool[slot // 8, (slot % 8) // 2, slot % 2] = jnp.concatenate(
                [r[:64], split_counts(r[64:65])], axis=0
            ).astype(BF)

    pl.semaphore_wait(barrier, len(dom_peers) + len(f_peers))

    m_r1 = send(pool.at[1 - core], r1, to_dom(partner))
    mrow = lambda i: mext.at[pl.ds(pl.multiple_of(i * 64, 64), 64), own]
    m_s1 = [
        send(mrow(f), mrow(f), to_feat(fy)),
        send(mrow(f), mrow(f), to_feat(fidx(zp, yl))),
        send(mrow(f), mrow(f), to_feat(fidx(zm, yl))),
    ]
    m_h = [
        send(mext.at[myrows, pl.ds(128, 128)], halo.at[f, 1], to_dom(dleft)),
        send(mext.at[myrows, pl.ds(2048, 128)], halo.at[f, 0], to_dom(dright)),
    ]

    t6[...] = jnp.zeros_like(t6)
    s6[...] = jnp.zeros_like(s6)
    ta, tb, tc = split3(tgt[...])
    sa, sb, sc = split3(src[:, pl.ds(pl.multiple_of(d * 256, 256), 256)])
    for k, (t, s) in enumerate([(ta, sa), (ta, sb), (tb, sa), (ta, sc), (tb, sb), (tc, sa)]):
        t6[k * 16:k * 16 + 10, :] = t
        s6[k * 16:k * 16 + 10, :] = s

    def score_step(j, peak):
        cols = pl.ds(pl.multiple_of(j * 512, 512), 512)
        s = jnp.maximum(dot(t6[:, cols], s6[...], ((0,), (0,))), 0.0)
        scores[cols, :] = s
        return jnp.maximum(peak, jnp.max(s.reshape(64, 8, 256), axis=0))

    peak = lax.fori_loop(0, 8, score_step, jnp.zeros((8, 256), F32))
    peak = jnp.max(peak, axis=0, keepdims=True)

    def add_blocks(blocks):
        total = blocks[0][...].astype(F32)
        for b in blocks[1:]:
            total = total + b[...].astype(F32)
        cnt = total[64:65] + total[65:66]
        return total[:64], cnt

    def packed(sums, cnt):
        return jnp.concatenate([sums, split_counts(cnt)], axis=0).astype(BF)

    m_r1.wait_recv()
    for xx in range(4):
        for yy in range(2):
            s1[xx, yy] = packed(*add_blocks([pool.at[core, xx, yy], r1.at[xx, yy]]))
    m_r2 = [
        send(s1.at[xp], r2.at[0], to_dom(x_peers[0])),
        send(s1.at[xm], r2.at[1], to_dom(x_peers[1])),
        send(s1.at[x2], r2.at[2], to_dom(x_peers[2])),
    ]

    m_s1[0].wait_recv()
    m_s2 = [
        send(mrow(fy), mrow(fy), to_feat(fidx(zp, yl))),
        send(mrow(fy), mrow(fy), to_feat(fidx(zm, yl))),
    ]
    for m in m_h:
        m.wait_recv()
    m_hf = [send(halo.at[f], halo.at[f], to_feat(p)) for p in f_peers]

    def exp_step(j, total):
        cols = pl.ds(pl.multiple_of(j * 512, 512), 512)
        e = jnp.exp(scores[cols, :] - peak)
        expo[cols, :] = e.astype(BF)
        return total + jnp.sum(e.reshape(64, 8, 256), axis=0)

    total = lax.fori_loop(0, 8, exp_step, jnp.zeros((8, 256), F32))
    inv = 1.0 / jnp.sum(total, axis=0, keepdims=True)

    for m in m_r2:
        m.wait_recv()
    for yy in range(2):
        s2[yy] = packed(*add_blocks([s1.at[x, yy]] + [r2.at[k, yy] for k in range(3)]))
    m_r3 = send(s2.at[1 - yh], r3, to_dom(yother))
    m_r3.wait_recv()
    sums, cnt = add_blocks([s2.at[yh], r3])
    pooled = sums / jnp.maximum(cnt, 1.0)
    pa, pb, pc = split3(pooled)
    wv = w_val[...]
    vals[d] = (dot(wv, pa) + dot(wv, pb) + dot(wv, pc)).astype(BF)

    def gather_start(buf):
        a = [send(buf(d), buf(d), to_dom(yother))]
        a += [send(buf(d), buf(d), to_dom(p)) for p in x_peers]
        return a, [send(buf(d), buf(d), to_dom(partner))]

    def gather_y(buf, a, p):
        a[0].wait_recv()
        b = [send(buf(yother), buf(yother), to_dom(i)) for i in x_peers]
        p.append(send(buf(yother), buf(yother), to_dom(partner)))
        return b

    x_from = [didx(yh, xm, core), didx(yh, xp, core), didx(yh, x2, core)]

    def gather_x(buf, msg, p, shift):
        for m, i in zip(msg, x_from):
            m.wait_recv()
            i = (i + shift) % 16
            p.append(send(buf(i), buf(i), to_dom(partner)))

    vslot = lambda i: vals.at[i]
    a, p = gather_start(vslot)
    b = gather_y(vslot, a, p)
    gather_x(vslot, a[1:], p, 0)
    gather_x(vslot, b, p, 8)
    for m in p:
        m.wait_recv()

    att = jnp.zeros((64, 256), F32)
    for k in range(16):
        att = att + dot(vals[k], expo[k * 256:(k + 1) * 256, :])
    ca[f] = (pooled + att * inv).astype(BF)
    m_ca = [send(ca.at[f], ca.at[f], to_feat(i)) for i in f_peers]

    def mhalf(i, h):
        return mext.at[pl.ds(pl.multiple_of(i * 64 + h * 32, 32), 32), own]

    m_s3 = []
    for m, i, h, to in (
        (m_s1[1], fidx(zm, yl), 0, zp),
        (m_s1[2], fidx(zp, yl), 1, zm),
        (m_s2[0], fidx(zm, 1 - yl), 0, zp),
        (m_s2[1], fidx(zp, 1 - yl), 1, zm),
    ):
        m.wait_recv()
        m_s3.append(send(mhalf(i, h), mhalf(i, h), to_feat(fidx(to, yl))))

    loc[0].wait()
    for m in m_ca:
        m.wait_recv()
    g = dot(wg[576:768, :], ca[...].reshape(512, 256)).astype(BF)
    gall[2 * d] = g[:, :128]
    gall[2 * d + 1] = g[:, 128:]
    gslot = lambda i: gall.at[pl.ds(2 * i, 2)]
    a, p = gather_start(gslot)

    for m in m_hf + m_s3:
        m.wait_recv()
    for i in range(8):
        mext[i * 64:(i + 1) * 64, 0:128] = halo[i, 0]
        mext[i * 64:(i + 1) * 64, 2176:2304] = halo[i, 1]
    b = gather_y(gslot, a, p)

    for c in range(9):
        cols = slice(c * 256, (c + 1) * 256)
        r = dot(wg[0:576, :], mext[:, cols])
        gsum[:, cols] = r[0:192]
        w1m[:, cols] = r[192:384]
        ubuf[:, cols] = r[384:576].astype(BF)

    gather_x(gslot, a[1:], p, 0)
    loc[1].wait()

    def diffuse(buf, t):
        lo, mid, hi = (buf[:, (t + k) * 128:(t + k + 1) * 128] for k in range(3))
        def pick(k):
            c = jnp.full((1, 128), adj_cols[t, k], jnp.int32)
            wlo, wmid, whi = ((c == t + i).astype(F32).astype(BF) for i in range(3))
            return lo * wlo + mid * wmid + hi * whi
        lhs = jnp.concatenate([lo, pick(1), pick(2), hi], axis=1)
        r = dot(lhs, adj[t])
        pos = lax.broadcasted_iota(jnp.int32, (1, 128), 1) + t * 128
        return r * (pos < nvalid).astype(F32)

    def first(t):
        cols = slice((t + 1) * 128, (t + 2) * 128)
        vbuf[:, cols] = (w1m[:, cols] + diffuse(ubuf, t)).astype(BF)

    def second(t):
        cols = slice((t + 1) * 128, (t + 2) * 128)
        gsum[:, cols] = gsum[:, cols] + diffuse(vbuf, t)

    first(0)
    first(15)
    tile = lambda i: vbuf.at[:, pl.ds(i * 128, 128)]
    m_v = [
        send(tile(1), tile(17), to_dom(dleft)),
        send(tile(16), tile(0), to_dom(dright)),
    ]
    for t in range(1, 15):
        first(t)
    gather_x(gslot, b, p, 8)
    for t in range(1, 15):
        second(t)
    for m in m_v:
        m.wait_recv()
    second(0)
    second(15)

    for m in p:
        m.wait_recv()
    loc[2].wait()

    def mix_step(s, carry):
        parts = []
        for h in range(2):
            t = s * 2 + h
            cols = [ccols[t, k] for k in range(2)]
            lhs = jnp.concatenate(
                [gall[c] for c in cols],
                axis=1,
            )
            parts.append(gall[t].astype(F32) + dot(lhs, ct[t]))
        gmix[s] = jnp.concatenate(parts, axis=1).astype(BF)
        return carry

    lax.fori_loop(0, 16, mix_step, 0)

    eye = lax.broadcasted_iota(jnp.int32, (64, 64), 0) == lax.broadcasted_iota(
        jnp.int32, (64, 64), 1
    )
    bcol = [
        jnp.sum(jnp.where(eye, bias[g:g + 1, :], 0.0), axis=1, keepdims=True) for g in range(3)
    ]
    win = w_in[...].astype(F32)

    for n in range(8):
        cols = slice(n * 256, (n + 1) * 256)
        ecols = slice(n * 256 + 128, (n + 1) * 256 + 128)
        hi_n = cluster[:, cols] >> 8
        oh = ohlo[:, cols]
        acc = dot(gmix[0], oh)
        for s in range(1, 16):
            acc = jnp.where(hi_n == s, dot(gmix[s], oh), acc)
        pre = acc + gsum[:, ecols]
        xi = xin[:, cols].astype(F32)
        terms = [
            win[g * 64:(g + 1) * 64, 0:1] * xi[0:1] + win[g * 64:(g + 1) * 64, 1:2] * xi[1:2]
            + bcol[g]
            for g in range(3)
        ]
        update = jax.nn.sigmoid(terms[0] + pre[0:64])
        reset = jax.nn.sigmoid(terms[1] + pre[64:128])
        cand = jnp.tanh(terms[2] + reset * pre[128:192])
        mk = (lax.broadcasted_iota(jnp.int32, (1, 256), 1) + n * 256 < nvalid).astype(F32)
        ms = state[:, cols].astype(F32) * mk
        out[:, cols] = ((update * ms + (1.0 - update) * cand) * mk).astype(BF)

    for m in msgs:
        m.wait_send()
    assert len(msgs) <= N_MSG


def body(
    state, inputs, adj_tiles, adj_cols, valid_rows, cluster_of, w_gates, w_input, bias, w_value,
    source_emb, target_emb, coarse_tiles, coarse_cols,
):
    wg = jnp.transpose(w_gates, (2, 0, 1, 3)).reshape(768, 512)
    vm = pl.BlockSpec(memory_space=pltpu.VMEM)
    sm = pl.BlockSpec(memory_space=pltpu.SMEM)
    hb = pl.BlockSpec(memory_space=pl.ANY)
    V = pltpu.VMEM
    return pl.pallas_call(
        kernel,
        out_shape=jax.ShapeDtypeStruct(state.shape, BF),
        in_specs=[vm, vm, hb, sm, sm, vm, hb, vm, vm, vm, vm, vm, hb, sm],
        out_specs=vm,
        scratch_shapes=[
            V((512, 2304), BF),
            V((8, 2, 64, 128), BF),
            V((256, 2048), BF),
            V((80, 2048), F32),
            V((1280, 2048), BF),
            V((2, 4, 2, 80, 256), BF),
            V((4, 2, 80, 256), BF),
            V((4, 2, 80, 256), BF),
            V((3, 2, 80, 256), BF),
            V((2, 80, 256), BF),
            V((80, 256), BF),
            V((96, 4096), BF),
            V((96, 256), BF),
            V((4096, 256), F32),
            V((4096, 256), BF),
            V((16, 64, 256), BF),
            V((8, 64, 256), BF),
            V((32, 192, 128), BF),
            V((16, 192, 256), BF),
            V((192, 2304), BF),
            V((192, 2304), BF),
            V((192, 2304), F32),
            V((192, 2304), F32),
            V((16, 512, 128), BF),
            V((768, 512), BF),
            V((32, 256, 128), BF),
            pltpu.SemaphoreType.DMA((N_MSG,)),
            pltpu.SemaphoreType.DMA((N_MSG,)),
            pltpu.SemaphoreType.DMA((3,)),
        ],
        compiler_params=pltpu.CompilerParams(collective_id=0, has_side_effects=True),
    )(
        state, inputs, adj_tiles.reshape(16, 512, 128), adj_cols, valid_rows,
        cluster_of.reshape(1, 2048), wg, w_input.reshape(192, 2), bias, w_value.reshape(64, 64),
        source_emb.reshape(10, 4096), target_emb.reshape(10, 4096),
        coarse_tiles.reshape(32, 256, 128), coarse_cols,
    )


def solution(mesh):
    return jax.shard_map(
        body,
        mesh=mesh,
        in_specs=(
            P("feat", "dom"),
            P(None, "dom"),
            P("dom", None, None, None),
            P("dom", None),
            P("dom"),
            P("dom"),
            P(None, "feat", None, None),
            P(None, "feat", None),
            P(None, "feat"),
            P("feat", None, None),
            P("feat", None, None),
            P("feat", None, None),
            P(),
            P(),
        ),
        out_specs=P("feat", "dom"),
        check_vma=False,
    )
```

time: 466 us -> 70.9 us (0.15)
  waiting for transfers between devices: 210 us -> 0 us
  matrix products: 110 us -> 0 us
  blocking collectives: 67.7 us -> 0 us
  Pallas kernels: 0 us -> 60 us
  local copies, waits for them, and re-layouts: 32 us -> 9.95 us
  other arithmetic: 21.6 us -> 0 us
  between operations: 14.5 us -> 0.66 us
  starting transfers between devices: 8.94 us -> 0 us
    all_gather x1 -> x0, waiting for transfers between devices: 168 us -> none  [body(): lax.all_gather(features, 'feat', axis=1, tiled=True)]
    dot_general x24 -> x0, matrix products: 110 us -> none  [the longest x8 57.3 us: one_block(): jnp.einsum('hei,hej->hij', source_block, target_emb, precision=lax.Precis...]
    psum x1 -> x0, blocking collectives: 67.7 us -> none  [body(): lax.psum(counts.astype(jnp.bfloat16), 'dom').astype(jnp.float32)]
    pallas_call x0 -> x1, Pallas kernels: none -> 60 us  [body(): pl.pallas_call(kernel, out_shape=jax.ShapeDtypeStruct(state.shape, BF), i...]
    psum x1 -> x0, waiting for transfers between devices: 41.8 us -> none  [body(): lax.psum(cluster_sums.astype(jnp.bfloat16), 'dom').astype(jnp.float32)]
    gather x5 -> x0, local copies, waits for them, and re-layouts: 14.2 us -> none  [the longest x2 9.23 us: body(): unpooled = jnp.take(coarse, cluster_of, axis=1)]
    reduce_sum x8 -> x0, other arithmetic: 12 us -> none  [one_block(): jnp.sum(raised, axis=2, keepdims=True)]
    ppermute x4 -> x0, starting transfers between devices: 8.87 us -> none  [the longest x2 7.39 us: extended_2(): after = lax.ppermute(leading, axis, down)]
  transfers between devices with their start and end apart: 6 -> 0, of which waited for: 2 -> 0; matrix products, arithmetic and copies ran while one was open for 5% -> 0% of each run, Pallas kernels for 0% -> 0%
where the time goes in v1:
time: 70.9 us; the launch traced here: 70.6 us
  Pallas kernels  60 us (85%)
  local copies, waits for them, and re-layouts  9.95 us (14%)
    pallas_call x1, Pallas kernels, body(): pl.pallas_call(kernel, out_shape=jax.ShapeDtypeStruct(state.shape, BF), i...  60 us
    unnamed x5, local copies, waits for them, and re-layouts  7.78 us
    transpose x1, local copies, waits for them, and re-layouts, body(): wg = jnp.transpose(w_gates, (2, 0, 1, 3)).reshape(768, 512)  2.17 us

profile of v1, /device:TPU:1, one launch (start us, length us, event | category | flops | bytes accessed | tf_op | source)
XLA Modules:
  0.0 70.6 jit_solution(3962173844946432103)
XLA Ops:
  0.7 1.4 %copy.17.adj_cols = s32[16,4]{1,0:T(8,128)} copy(s32[16,4]{0,1:T(4,128)} %param.17) | data formatting | bytes 512 | tf_op args[3]
  2.0 1.4 %copy.18.ccols = s32[32,2]{1,0:T(8,128)} copy(s32[32,2]{0,1:T(2,128)} %param.27) | data formatting | bytes 512 | tf_op args[13]
  3.4 1.4 %copy.16 = bf16[3,64,2]{2,1,0:T(8,128)(2,1)} copy(bf16[3,64,2]{1,2,0:T(2,128)(2,1)} %param.21) | data formatting | bytes 1536 | tf_op args[7]
  4.8 2.0 %copy_bitcast_fusion = (f32[10,4096]{1,0:T(8,128)}, f32[10,4096]{1,0:T(8,128)}) fusion(f32[1,10,4096]{2,0,1:T(1,128)} %param.25, f32[1,10,4096]{2,0,1:T(1,128)} %param.24), kind=kLoop, calls=%fused_computation | loop fusion | bytes 655360
  6.8 2.2 %copy.15 = bf16[4,3,64,512]{3,2,1,0:T(8,128)(2,1)} copy(bf16[4,3,64,512]{3,0,2,1:T(4,128)(2,1)} %bitcast.14) | data formatting | bytes 1572864 | tf_op jit(solution)/shard_map/transpose | solution.py:361
  8.9 60.0 %shard_map.136 = bf16[64,2048]{1,0:T(8,128)(2,1)} custom-call(bf16[64,2048]{1,0:T(8,128)(2,1)} %state.1, bf16[2,2048]{1,0:T(2,128)(2,1)} %xin.1, bf16[16,512,128]{2,1,0:T(8,128)(2,1)} %bitcast.12, s32[16,4]{1,0:T(8,128)} %copy.17.adj_cols, s32[1]{0:T(128)S(6)} %copy.24.valid, s32[1,2048]{1,0:T(1,128)} %bitcast.17, bf16[768,512]{1,0:T(8,128)(2,1)} %bitcast.11, ...), custom_call_target="tpu_custom_call" | custom-call | tf_op jit(solution)/shard_map/pallas_call | solution.py:366
  68.9 1.7 %copy.25 = bf16[64,2048]{1,0:T(8,128)(2,1)} copy(bf16[64,2048]{1,0:T(8,128)(2,1)} %shard_map.136) | data formatting | bytes 524288

commit v2 on v1

v2 whole, which is shorter than its diff:
```python
import jax
import jax.numpy as jnp
from jax import lax
from jax.experimental import pallas as pl
from jax.experimental.pallas import tpu as pltpu
from jax.sharding import PartitionSpec as P

MESH = pl.DeviceIdType.MESH
BF = jnp.bfloat16
F32 = jnp.float32
N_MSG = 80


def dot(a, b, dims=((1,), (0,))):
    return lax.dot_general(a, b, (dims, ((), ())), preferred_element_type=F32)


def split3(v):
    a = v.astype(BF)
    r = v - a.astype(F32)
    b = r.astype(BF)
    c = (r - b.astype(F32)).astype(BF)
    return a, b, c


def split_counts(total):
    high = jnp.floor(total * (1.0 / 256.0)) * 256.0
    low = total - high
    row = lax.broadcasted_iota(jnp.int32, (16, total.shape[1]), 0)
    return jnp.where(row == 0, high, jnp.where(row == 1, low, 0.0))


def kernel(
    state, xin, adj_hbm, adj_cols, valid, cluster, wg_hbm, w_in, bias, w_val, src_hbm, tgt_hbm,
    ct_hbm, ccols, out,
    mext, halo, ohlo, base, pl_lhs, pool, r1, s1, r2, s2, r3, src, tgt, t6, s6, scores, expo,
    vals, pooled, ca, gall, gmix, ubuf, vbuf, w1m, gsum, adj, wraw, wg, ct,
    ssem, rsem, lsem,
):
    d = lax.axis_index("dom")
    f = lax.axis_index("feat")
    core, x, yh = d % 2, (d // 2) % 4, d // 8
    z, yl = f // 2, f % 2
    xp, xm, x2 = (x + 1) % 4, (x + 3) % 4, (x + 2) % 4
    zp, zm = (z + 1) % 4, (z + 3) % 4
    q, qp, qm, q2 = (i * 2 + core for i in (x, xp, xm, x2))
    dev = lambda i: (i, f)
    fdev = lambda i: (d, i)
    partner, yother = dev(d + 1 - 2 * core), dev((d + 8) % 16)
    dxp, dxm, dx2 = (dev(yh * 8 + i) for i in (qp, qm, q2))
    dleft, dright = dev((d + 15) % 16), dev((d + 1) % 16)
    fi = lambda a, b: a * 2 + b
    fy, fzp, fzm = f + 1 - 2 * yl, fi(zp, yl), fi(zm, yl)
    f_peers = [fdev((f + k) % 8) for k in range(1, 8)]

    msgs = []

    def send(src_ref, dst_ref, to):
        i = len(msgs)
        cp = pltpu.make_async_remote_copy(
            src_ref=src_ref, dst_ref=dst_ref, send_sem=ssem.at[i], recv_sem=rsem.at[i],
            device_id=to, device_id_type=MESH,
        )
        cp.start()
        msgs.append(cp)
        return cp

    same = lambda ref, to: send(ref, ref, to)

    mine = pl.ds(pl.multiple_of(d * 256, 256), 256)
    loc = [
        pltpu.make_async_copy(wg_hbm, wraw, lsem.at[0]),
        pltpu.make_async_copy(adj_hbm, adj, lsem.at[1]),
        pltpu.make_async_copy(ct_hbm, ct, lsem.at[2]),
    ]
    emb = []
    for r in range(10):
        emb.append(pltpu.make_async_copy(tgt_hbm.at[r], tgt.at[pl.ds(r, 1)], lsem.at[3 + r]))
        emb.append(
            pltpu.make_async_copy(src_hbm.at[r, :, mine], src.at[pl.ds(r, 1)], lsem.at[13 + r])
        )
    for c in emb + loc:
        c.start()

    barrier = pltpu.get_barrier_semaphore()
    cross = dev((d + 15 + 2 * core) % 16)
    peers = [partner, cross, yother, dxp, dxm, dx2] + f_peers
    for p in peers:
        pl.semaphore_signal(barrier, inc=1, device_id=p, device_id_type=MESH)

    nvalid = valid[0]
    mask = (lax.broadcasted_iota(jnp.int32, (1, 2048), 1) < nvalid).astype(F32)
    masked32 = state[...].astype(F32) * mask
    myrows = pl.ds(pl.multiple_of(f * 64, 64), 64)
    own = pl.ds(128, 2048)
    mext[myrows, own] = masked32.astype(BF)
    base[0:64, :] = masked32
    row16 = lax.broadcasted_iota(jnp.int32, (16, 2048), 0)
    base[64:80, :] = jnp.where(row16 == 0, mask, 0.0)
    low = cluster[...] & 255
    high = cluster[...] >> 8
    ohlo[...] = (lax.broadcasted_iota(jnp.int32, (256, 2048), 0) == low).astype(F32).astype(BF)

    def pool_part(c, to_core):
        for xx in range(4):
            for yy in range(2):
                slot = xx * 2 + yy
                hit = high == (yy * 8 + xx * 2) + to_core
                pl_lhs[slot * 80:(slot + 1) * 80, :] = jnp.where(hit, base[...], 0.0).astype(BF)
        for i in range(2):
            res = dot(pl_lhs[i * 320:(i + 1) * 320, :], ohlo[...], ((1,), (1,)))
            for k in range(4):
                slot = i * 4 + k
                r = res[k * 80:(k + 1) * 80]
                pool[c, slot // 2, slot % 2] = jnp.concatenate(
                    [r[:64], split_counts(r[64:65])], axis=0
                ).astype(BF)

    pool_part(0, 1 - core)

    pl.semaphore_wait(barrier, len(peers))

    m_r1 = send(pool.at[0], r1, partner)
    mrow = lambda i: mext.at[pl.ds(pl.multiple_of(i * 64, 64), 64), own]
    m_s1 = [same(mrow(f), fdev(i)) for i in (fy, fzp, fzm)]
    m_h = [
        send(mext.at[myrows, pl.ds(128, 128)], halo.at[f, 1], dleft),
        send(mext.at[myrows, pl.ds(2048, 128)], halo.at[f, 0], dright),
    ]
    pool_part(1, core)

    for c in emb:
        c.wait()
    t6[...] = jnp.zeros_like(t6)
    s6[...] = jnp.zeros_like(s6)
    ta, tb, tc = split3(tgt[0:10, :])
    sa, sb, sc = split3(src[0:10, :])
    for k, (t, s) in enumerate([(ta, sa), (ta, sb), (tb, sa), (ta, sc), (tb, sb), (tc, sa)]):
        t6[k * 16:k * 16 + 10, :] = t
        s6[k * 16:k * 16 + 10, :] = s

    def score_step(j, peak):
        cols = pl.ds(pl.multiple_of(j * 512, 512), 512)
        s = jnp.maximum(dot(t6[:, cols], s6[...], ((0,), (0,))), 0.0)
        scores[cols, :] = s
        return jnp.maximum(peak, jnp.max(s.reshape(64, 8, 256), axis=0))

    def add_blocks(blocks):
        total = blocks[0][...].astype(F32)
        for b in blocks[1:]:
            total = total + b[...].astype(F32)
        return total[:64], total[64:65] + total[65:66]

    def packed(sums, cnt):
        return jnp.concatenate([sums, split_counts(cnt)], axis=0).astype(BF)

    m_r1.wait_recv()
    for xx in range(4):
        for yy in range(2):
            s1[xx, yy] = packed(*add_blocks([pool.at[1, xx, yy], r1.at[xx, yy]]))
    m_r2 = [
        send(s1.at[x2], r2.at[2], dx2),
        send(s1.at[xp], r2.at[0], dxp),
        send(s1.at[xm], r2.at[1], dxm),
    ]

    peak = lax.fori_loop(0, 8, score_step, jnp.zeros((8, 256), F32))
    peak = jnp.max(peak, axis=0, keepdims=True)

    for m in m_r2:
        m.wait_recv()
    for yy in range(2):
        s2[yy] = packed(*add_blocks([s1.at[x, yy]] + [r2.at[k, yy] for k in range(3)]))
    m_r3 = send(s2, r3, yother)

    m_s1[0].wait_recv()
    m_s2 = [same(mrow(fy), fdev(i)) for i in (fzp, fzm)]
    for m in m_h:
        m.wait_recv()
    m_hf = [same(halo.at[f], p) for p in f_peers]

    def exp_step(j, total):
        cols = pl.ds(pl.multiple_of(j * 512, 512), 512)
        e = jnp.exp(scores[cols, :] - peak)
        expo[cols, :] = e.astype(BF)
        return total + jnp.sum(e.reshape(64, 8, 256), axis=0)

    total = lax.fori_loop(0, 8, exp_step, jnp.zeros((8, 256), F32))
    inv = 1.0 / jnp.sum(total, axis=0, keepdims=True)

    m_r3.wait_recv()
    wv = w_val[...]
    for yy in range(2):
        sums, cnt = add_blocks([s2.at[yy], r3.at[yy]])
        avg = sums / jnp.maximum(cnt, 1.0)
        pooled[yy] = avg
        pa, pb, pc = split3(avg)
        vals[q, yy] = (dot(wv, pa) + dot(wv, pb) + dot(wv, pc)).astype(BF)

    m_v = [same(vals.at[q], dxp), same(vals.at[q], dxm)]
    pv = [same(vals.at[q], partner)]
    m_v[0].wait_recv()
    m_v.append(same(vals.at[qm, 0], dxp))
    pv.append(same(vals.at[qm], partner))
    m_v[1].wait_recv()
    m_v.append(same(vals.at[qp, 1], dxm))
    pv.append(same(vals.at[qp], partner))
    mhalf = lambda i, h: mext.at[pl.ds(pl.multiple_of(i * 64 + h * 32, 32), 32), own]
    m_s1[1].wait_recv()
    m_s3 = [same(mhalf(fzm, 0), fdev(fzp))]
    m_s1[2].wait_recv()
    m_s3.append(same(mhalf(fzp, 1), fdev(fzm)))
    for h in range(2):
        m_v[2 + h].wait_recv()
        pv.append(same(vals.at[q2, h], partner))
    for m in pv:
        m.wait_recv()

    att = jnp.zeros((64, 256), F32)
    for k in range(16):
        att = att + dot(vals[k % 8, k // 8], expo[k * 256:(k + 1) * 256, :])
    ca[f] = (pooled[yh] + att * inv).astype(BF)
    m_ca = [same(ca.at[f], p) for p in f_peers]

    loc[0].wait()
    for k in range(4):
        wg[k * 192:(k + 1) * 192, :] = wraw[:, k, :]
    for m in m_ca:
        m.wait_recv()
    g = dot(wg[576:768, :], ca[...].reshape(512, 256)).astype(BF)
    gall[2 * d] = g[:, :128]
    gall[2 * d + 1] = g[:, 128:]
    gs = lambda a, b: gall.at[pl.ds(2 * (a * 8 + b), 2)]
    yo = 1 - yh
    g_y = same(gs(yh, q), yother)
    g_a = [same(gs(yh, q), dxp), same(gs(yh, q), dxm)]
    pg = [same(gs(yh, q), partner)]

    m_s2[0].wait_recv()
    m_s3.append(same(mhalf(fi(zm, 1 - yl), 0), fdev(fzp)))
    m_s2[1].wait_recv()
    m_s3.append(same(mhalf(fi(zp, 1 - yl), 1), fdev(fzm)))
    g_y.wait_recv()
    g_b = [same(gs(yo, q), dxp), same(gs(yo, q), dxm)]
    pg.append(same(gs(yo, q), partner))
    g_a[0].wait_recv()
    g_f = [same(gs(yh, qm), dxp)]
    pg.append(same(gs(yh, qm), partner))
    g_a[1].wait_recv()
    pg.append(same(gs(yh, qp), partner))

    for m in m_hf + m_s3:
        m.wait_recv()
    for i in range(8):
        mext[i * 64:(i + 1) * 64, 0:128] = halo[i, 0]
        mext[i * 64:(i + 1) * 64, 2176:2304] = halo[i, 1]

    for c in range(9):
        cols = slice(c * 256, (c + 1) * 256)
        r = dot(wg[0:576, :], mext[:, cols])
        gsum[:, cols] = r[0:192]
        w1m[:, cols] = r[192:384]
        ubuf[:, cols] = r[384:576].astype(BF)

    g_b[0].wait_recv()
    pg.append(same(gs(yo, qm), partner))
    g_b[1].wait_recv()
    g_f.append(same(gs(yo, qp), dxm))
    pg.append(same(gs(yo, qp), partner))
    loc[1].wait()

    def diffuse(buf, t):
        lo, mid, hi = (buf[:, (t + k) * 128:(t + k + 1) * 128] for k in range(3))

        def pick(k):
            c = jnp.full((1, 128), adj_cols[k, t], jnp.int32)
            wlo, wmid, whi = ((c == t + i).astype(F32).astype(BF) for i in range(3))
            return lo * wlo + mid * wmid + hi * whi

        lhs = jnp.concatenate([lo, pick(1), pick(2), hi], axis=1)
        r = dot(lhs, adj[t])
        pos = lax.broadcasted_iota(jnp.int32, (1, 128), 1) + t * 128
        return r * (pos < nvalid).astype(F32)

    def first(t):
        cols = slice((t + 1) * 128, (t + 2) * 128)
        vbuf[:, cols] = (w1m[:, cols] + diffuse(ubuf, t)).astype(BF)

    def second(t):
        cols = slice((t + 1) * 128, (t + 2) * 128)
        gsum[:, cols] = gsum[:, cols] + diffuse(vbuf, t)

    first(0)
    first(15)
    tile = lambda i: vbuf.at[:, pl.ds(i * 128, 128)]
    m_vh = [send(tile(1), tile(17), dleft), send(tile(16), tile(0), dright)]
    for t in range(1, 15):
        first(t)
    g_f[0].wait_recv()
    pg.append(same(gs(yh, q2), partner))
    g_f[1].wait_recv()
    pg.append(same(gs(yo, q2), partner))
    for t in range(1, 15):
        second(t)
    for m in m_vh:
        m.wait_recv()
    second(0)
    second(15)

    for m in pg:
        m.wait_recv()
    loc[2].wait()

    for s in range(16):
        parts = []
        for t in (2 * s, 2 * s + 1):
            lhs = jnp.concatenate([gall[ccols[k, t]] for k in range(2)], axis=1)
            parts.append(gall[t].astype(F32) + dot(lhs, ct[t]))
        gmix[s] = jnp.concatenate(parts, axis=1).astype(BF)

    eye = lax.broadcasted_iota(jnp.int32, (64, 64), 0) == lax.broadcasted_iota(
        jnp.int32, (64, 64), 1
    )
    column = lambda row: jnp.sum(jnp.where(eye, row, 0.0), axis=1, keepdims=True)
    bcol = [column(bias[g:g + 1, :]) for g in range(3)]
    win = [w_in[g].astype(F32) for g in range(3)]
    wcol = [[column(win[g][i:i + 1]) for i in range(2)] for g in range(3)]

    for n in range(8):
        cols = slice(n * 256, (n + 1) * 256)
        ecols = slice(n * 256 + 128, (n + 1) * 256 + 128)
        hi_n = cluster[:, cols] >> 8
        oh = ohlo[:, cols]
        acc = dot(gmix[0], oh)
        for s in range(1, 16):
            acc = jnp.where(hi_n == s, dot(gmix[s], oh), acc)
        pre = acc + gsum[:, ecols]
        xi = xin[:, cols].astype(F32)
        terms = [wcol[g][0] * xi[0:1] + wcol[g][1] * xi[1:2] + bcol[g] for g in range(3)]
        update = jax.nn.sigmoid(terms[0] + pre[0:64])
        reset = jax.nn.sigmoid(terms[1] + pre[64:128])
        cand = jnp.tanh(terms[2] + reset * pre[128:192])
        mk = (lax.broadcasted_iota(jnp.int32, (1, 256), 1) + n * 256 < nvalid).astype(F32)
        ms = state[:, cols].astype(F32) * mk
        out[:, cols] = ((update * ms + (1.0 - update) * cand) * mk).astype(BF)

    for m in msgs:
        m.wait_send()
    assert len(msgs) <= N_MSG


def body(
    state, inputs, adj_tiles, adj_cols, valid_rows, cluster_of, w_gates, w_input, bias, w_value,
    source_emb, target_emb, coarse_tiles, coarse_cols,
):
    vm = pl.BlockSpec(memory_space=pltpu.VMEM)
    sm = pl.BlockSpec(memory_space=pltpu.SMEM)
    hb = pl.BlockSpec(memory_space=pl.ANY)
    V = pltpu.VMEM
    return pl.pallas_call(
        kernel,
        out_shape=jax.ShapeDtypeStruct(state.shape, BF),
        in_specs=[vm, vm, hb, sm, sm, vm, hb, vm, vm, vm, hb, hb, hb, sm],
        out_specs=vm,
        scratch_shapes=[
            V((512, 2304), BF),
            V((8, 2, 64, 128), BF),
            V((256, 2048), BF),
            V((80, 2048), F32),
            V((640, 2048), BF),
            V((2, 4, 2, 80, 256), BF),
            V((4, 2, 80, 256), BF),
            V((4, 2, 80, 256), BF),
            V((3, 2, 80, 256), BF),
            V((2, 80, 256), BF),
            V((2, 80, 256), BF),
            V((16, 256), F32),
            V((16, 4096), F32),
            V((96, 4096), BF),
            V((96, 256), BF),
            V((4096, 256), F32),
            V((4096, 256), BF),
            V((8, 2, 64, 256), BF),
            V((2, 64, 256), F32),
            V((8, 64, 256), BF),
            V((32, 192, 128), BF),
            V((16, 192, 256), BF),
            V((192, 2304), BF),
            V((192, 2304), BF),
            V((192, 2304), F32),
            V((192, 2304), F32),
            V((16, 512, 128), BF),
            V((192, 4, 512), BF),
            V((768, 512), BF),
            V((32, 256, 128), BF),
            pltpu.SemaphoreType.DMA((N_MSG,)),
            pltpu.SemaphoreType.DMA((N_MSG,)),
            pltpu.SemaphoreType.DMA((23,)),
        ],
        compiler_params=pltpu.CompilerParams(collective_id=0, has_side_effects=True),
    )(
        state, inputs, adj_tiles.reshape(16, 512, 128), adj_cols.T, valid_rows,
        cluster_of.reshape(1, 2048), w_gates.reshape(192, 4, 512),
        jnp.transpose(w_input, (0, 2, 1)), bias, w_value.reshape(64, 64),
        jnp.transpose(source_emb, (1, 0, 2)), jnp.transpose(target_emb, (1, 0, 2)),
        coarse_tiles.reshape(32, 256, 128), coarse_cols.T,
    )


def solution(mesh):
    return jax.shard_map(
        body,
        mesh=mesh,
        in_specs=(
            P("feat", "dom"),
            P(None, "dom"),
            P("dom", None, None, None),
            P("dom", None),
            P("dom"),
            P("dom"),
            P(None, "feat", None, None),
            P(None, "feat", None),
            P(None, "feat"),
            P("feat", None, None),
            P("feat", None, None),
            P("feat", None, None),
            P(),
            P(),
        ),
        out_specs=P("feat", "dom"),
        check_vma=False,
    )
```

time: 70.9 us -> 59.8 us (0.84)
  the two profiles are of different devices: /device:TPU:1 before, /device:TPU:7 now
where the time goes in v2:
time: 59.8 us; the launch traced here: 59.7 us
  Pallas kernels  57.3 us (96%)
  local copies, waits for them, and re-layouts  1.67 us (3%)
  between operations  0.66 us (1%)
    pallas_call x1, Pallas kernels, body(): pl.pallas_call(kernel, out_shape=jax.ShapeDtypeStruct(state.shape, BF), i...  57.3 us
    unnamed x1, local copies, waits for them, and re-layouts  1.67 us

profile of v2, /device:TPU:7, one launch (start us, length us, event | category | flops | bytes accessed | tf_op | source)
XLA Modules:
  0.0 59.7 jit_solution(8138221643183084954)
XLA Ops:
  0.7 57.3 %shard_map.136 = bf16[64,2048]{1,0:T(8,128)(2,1)} custom-call(bf16[64,2048]{1,0:T(8,128)(2,1)} %state.1, bf16[2,2048]{1,0:T(2,128)(2,1)} %xin.1, bf16[16,512,128]{2,1,0:T(8,128)(2,1)} %bitcast.10, s32[4,16]{1,0:T(4,128)} %bitcast.17, s32[1]{0:T(128)S(6)} %copy.16.valid, s32[1,2048]{1,0:T(1,128)} %bitcast.16, bf16[192,4,512]{2,1,0:T(4,128)(2,1)} %bitcast.12, ...), custom_call_target="tpu_custom_call" | custom-call | tf_op jit(solution)/shard_map/pallas_call | solution.py:360
  58.0 1.7 %copy.17 = bf16[64,2048]{1,0:T(8,128)(2,1)} copy(bf16[64,2048]{1,0:T(8,128)(2,1)} %shard_map.136) | data formatting | bytes 524288

commit v3 on v2

--- a/solution.py
+++ b/solution.py
@@ -8,7 +8,7 @@
 MESH = pl.DeviceIdType.MESH
 BF = jnp.bfloat16
 F32 = jnp.float32
-N_MSG = 80
+N_MSG = 28
 
 
 def dot(a, b, dims=((1,), (0,))):
@@ -32,9 +32,9 @@
 
 def kernel(
     state, xin, adj_hbm, adj_cols, valid, cluster, wg_hbm, w_in, bias, w_val, src_hbm, tgt_hbm,
-    ct_hbm, ccols, out,
-    mext, halo, ohlo, base, pl_lhs, pool, r1, s1, r2, s2, r3, src, tgt, t6, s6, scores, expo,
-    vals, pooled, ca, gall, gmix, ubuf, vbuf, w1m, gsum, adj, wraw, wg, ct,
+    ct_hbm, ccols, out_hbm,
+    mext, ohlo, base, pl_lhs, pool, r1, s1, r2, s2, r3, src, tgt, t6, s6, scores, expo,
+    vals, pooled, ca, gall0, gall1, gall2, gmix, ubuf, vbuf, w1m, gsum, out, adj, wraw, wg, ct,
     ssem, rsem, lsem,
 ):
     d = lax.axis_index("dom")
@@ -48,24 +48,38 @@
     fdev = lambda i: (d, i)
     partner, yother = dev(d + 1 - 2 * core), dev((d + 8) % 16)
     dxp, dxm, dx2 = (dev(yh * 8 + i) for i in (qp, qm, q2))
+    rq, rqp, rqm, rq2 = (i * 2 + 1 - core for i in (x, xp, xm, x2))
+    pxp, pxm = (dev(yh * 8 + i) for i in (rqp, rqm))
     dleft, dright = dev((d + 15) % 16), dev((d + 1) % 16)
     fi = lambda a, b: a * 2 + b
     fy, fzp, fzm = f + 1 - 2 * yl, fi(zp, yl), fi(zm, yl)
     f_peers = [fdev((f + k) % 8) for k in range(1, 8)]
 
-    msgs = []
-
-    def send(src_ref, dst_ref, to):
-        i = len(msgs)
-        cp = pltpu.make_async_remote_copy(
-            src_ref=src_ref, dst_ref=dst_ref, send_sem=ssem.at[i], recv_sem=rsem.at[i],
-            device_id=to, device_id_type=MESH,
-        )
-        cp.start()
-        msgs.append(cp)
-        return cp
-
-    same = lambda ref, to: send(ref, ref, to)
+    groups = []
+
+    class Group:
+        def __init__(self, whole):
+            self.whole, self.sems = whole, (ssem.at[len(groups)], rsem.at[len(groups)])
+            groups.append(self)
+
+        def copy(self, src_ref, dst_ref, to):
+            return pltpu.make_async_remote_copy(
+                src_ref=src_ref, dst_ref=dst_ref, send_sem=self.sems[0], recv_sem=self.sems[1],
+                device_id=to, device_id_type=MESH,
+            )
+
+        def send(self, src_ref, dst_ref, to):
+            self.copy(src_ref, dst_ref, to).start()
+
+        def same(self, ref, *to):
+            for i in to:
+                self.send(ref, ref, i)
+
+        def recv(self):
+            self.copy(self.whole, self.whole, partner).wait_recv()
+
+        def sent(self):
+            self.copy(self.whole, self.whole, partner).wait_send()
 
     mine = pl.ds(pl.multiple_of(d * 256, 256), 256)
     loc = [
@@ -84,7 +98,7 @@
 
     barrier = pltpu.get_barrier_semaphore()
     cross = dev((d + 15 + 2 * core) % 16)
-    peers = [partner, cross, yother, dxp, dxm, dx2] + f_peers
+    peers = [partner, cross, yother, dxp, dxm, dx2, pxp, pxm] + f_peers
     for p in peers:
         pl.semaphore_signal(barrier, inc=1, device_id=p, device_id_type=MESH)
 
@@ -120,13 +134,11 @@
 
     pl.semaphore_wait(barrier, len(peers))
 
-    m_r1 = send(pool.at[0], r1, partner)
-    mrow = lambda i: mext.at[pl.ds(pl.multiple_of(i * 64, 64), 64), own]
-    m_s1 = [same(mrow(f), fdev(i)) for i in (fy, fzp, fzm)]
-    m_h = [
-        send(mext.at[myrows, pl.ds(128, 128)], halo.at[f, 1], dleft),
-        send(mext.at[myrows, pl.ds(2048, 128)], halo.at[f, 0], dright),
-    ]
+    m_r1 = Group(r1)
+    m_r1.send(pool.at[0], r1, partner)
+    m_h = Group(mext.at[0:64, 0:256])
+    m_h.send(mext.at[myrows, pl.ds(128, 128)], mext.at[myrows, pl.ds(2176, 128)], dleft)
+    m_h.send(mext.at[myrows, pl.ds(2048, 128)], mext.at[myrows, pl.ds(0, 128)], dright)
     pool_part(1, core)
 
     for c in emb:
@@ -154,30 +166,24 @@
     def packed(sums, cnt):
         return jnp.concatenate([sums, split_counts(cnt)], axis=0).astype(BF)
 
-    m_r1.wait_recv()
+    m_r1.recv()
     for xx in range(4):
         for yy in range(2):
             s1[xx, yy] = packed(*add_blocks([pool.at[1, xx, yy], r1.at[xx, yy]]))
-    m_r2 = [
-        send(s1.at[x2], r2.at[2], dx2),
-        send(s1.at[xp], r2.at[0], dxp),
-        send(s1.at[xm], r2.at[1], dxm),
-    ]
-
-    peak = lax.fori_loop(0, 8, score_step, jnp.zeros((8, 256), F32))
+    m_r2 = Group(r2)
+    m_r2.send(s1.at[x2], r2.at[2], dx2)
+    m_r2.send(s1.at[xp], r2.at[0], dxp)
+    m_r2.send(s1.at[xm], r2.at[1], dxm)
+
+    peak = lax.fori_loop(0, 4, score_step, jnp.zeros((8, 256), F32))
+    m_h.recv()
+    mrow = lambda i: mext.at[pl.ds(pl.multiple_of(i * 64, 64), 64), :]
+    mhalf = lambda i, h: mext.at[pl.ds(pl.multiple_of(i * 64 + h * 32, 32), 32), :]
+    st_y, st_z = Group(mext.at[0:64]), Group(mext.at[0:128])
+    st_y.same(mrow(f), fdev(fy))
+    st_z.same(mrow(f), fdev(fzp), fdev(fzm))
+    peak = lax.fori_loop(4, 8, score_step, peak)
     peak = jnp.max(peak, axis=0, keepdims=True)
-
-    for m in m_r2:
-        m.wait_recv()
-    for yy in range(2):
-        s2[yy] = packed(*add_blocks([s1.at[x, yy]] + [r2.at[k, yy] for k in range(3)]))
-    m_r3 = send(s2, r3, yother)
-
-    m_s1[0].wait_recv()
-    m_s2 = [same(mrow(fy), fdev(i)) for i in (fzp, fzm)]
-    for m in m_h:
-        m.wait_recv()
-    m_hf = [same(halo.at[f], p) for p in f_peers]
 
     def exp_step(j, total):
         cols = pl.ds(pl.multiple_of(j * 512, 512), 512)
@@ -188,7 +194,19 @@
     total = lax.fori_loop(0, 8, exp_step, jnp.zeros((8, 256), F32))
     inv = 1.0 / jnp.sum(total, axis=0, keepdims=True)
 
-    m_r3.wait_recv()
+    m_r2.recv()
+    for yy in range(2):
+        s2[yy] = packed(*add_blocks([s1.at[x, yy]] + [r2.at[k, yy] for k in range(3)]))
+    m_r3 = Group(s2)
+    m_r3.send(s2, r3, yother)
+
+    st_y.recv()
+    st_yz = Group(mext.at[0:128])
+    st_yz.same(mrow(fy), fdev(fzp), fdev(fzm))
+    loc[0].wait()
+    for k in range(4):
+        wg[k * 192:(k + 1) * 192, :] = wraw[:, k, :]
+    m_r3.recv()
     wv = w_val[...]
     for yy in range(2):
         sums, cnt = add_blocks([s2.at[yy], r3.at[yy]])
@@ -197,64 +215,41 @@
         pa, pb, pc = split3(avg)
         vals[q, yy] = (dot(wv, pa) + dot(wv, pb) + dot(wv, pc)).astype(BF)
 
-    m_v = [same(vals.at[q], dxp), same(vals.at[q], dxm)]
-    pv = [same(vals.at[q], partner)]
-    m_v[0].wait_recv()
-    m_v.append(same(vals.at[qm, 0], dxp))
-    pv.append(same(vals.at[qm], partner))
-    m_v[1].wait_recv()
-    m_v.append(same(vals.at[qp, 1], dxm))
-    pv.append(same(vals.at[qp], partner))
-    mhalf = lambda i, h: mext.at[pl.ds(pl.multiple_of(i * 64 + h * 32, 32), 32), own]
-    m_s1[1].wait_recv()
-    m_s3 = [same(mhalf(fzm, 0), fdev(fzp))]
-    m_s1[2].wait_recv()
-    m_s3.append(same(mhalf(fzp, 1), fdev(fzm)))
-    for h in range(2):
-        m_v[2 + h].wait_recv()
-        pv.append(same(vals.at[q2, h], partner))
-    for m in pv:
-        m.wait_recv()
-
-    att = jnp.zeros((64, 256), F32)
-    for k in range(16):
-        att = att + dot(vals[k % 8, k // 8], expo[k * 256:(k + 1) * 256, :])
+    m_v, m_pv = Group(vals.at[0:2]), Group(vals.at[0:3])
+    m_v.same(vals.at[q], dxp, dxm)
+    m_pv.same(vals.at[q], partner)
+
+    def attend(total, i, halves=(0, 1)):
+        for yy in halves:
+            rows = pl.ds(pl.multiple_of((yy * 8 + i) * 256, 256), 256)
+            total = total + dot(vals[i, yy], expo[rows, :])
+        return total
+
+    att = attend(jnp.zeros((64, 256), F32), q)
+    st_z.recv()
+    st_far = Group(mext.at[0:128])
+    st_far.same(mhalf(fzm, 0), fdev(fzp))
+    st_far.same(mhalf(fzp, 1), fdev(fzm))
+    m_v.recv()
+    m_far = Group(vals.at[0:2])
+    m_far.same(vals.at[qm, 0], dxp, pxp)
+    m_far.same(vals.at[qp, 1], dxm, pxm)
+    m_pv.same(vals.at[qm], partner)
+    m_pv.same(vals.at[qp], partner)
+    att = attend(attend(att, qm), qp)
+    m_pv.recv()
+    for i in (rq, rqm, rqp):
+        att = attend(att, i)
+    st_yz.recv()
+    st_far.same(mhalf(fi(zm, 1 - yl), 0), fdev(fzp))
+    st_far.same(mhalf(fi(zp, 1 - yl), 1), fdev(fzm))
+    m_far.recv()
+    att = attend(attend(att, q2), rq2)
     ca[f] = (pooled[yh] + att * inv).astype(BF)
-    m_ca = [same(ca.at[f], p) for p in f_peers]
-
-    loc[0].wait()
-    for k in range(4):
-        wg[k * 192:(k + 1) * 192, :] = wraw[:, k, :]
-    for m in m_ca:
-        m.wait_recv()
-    g = dot(wg[576:768, :], ca[...].reshape(512, 256)).astype(BF)
-    gall[2 * d] = g[:, :128]
-    gall[2 * d + 1] = g[:, 128:]
-    gs = lambda a, b: gall.at[pl.ds(2 * (a * 8 + b), 2)]
-    yo = 1 - yh
-    g_y = same(gs(yh, q), yother)
-    g_a = [same(gs(yh, q), dxp), same(gs(yh, q), dxm)]
-    pg = [same(gs(yh, q), partner)]
-
-    m_s2[0].wait_recv()
-    m_s3.append(same(mhalf(fi(zm, 1 - yl), 0), fdev(fzp)))
-    m_s2[1].wait_recv()
-    m_s3.append(same(mhalf(fi(zp, 1 - yl), 1), fdev(fzm)))
-    g_y.wait_recv()
-    g_b = [same(gs(yo, q), dxp), same(gs(yo, q), dxm)]
-    pg.append(same(gs(yo, q), partner))
-    g_a[0].wait_recv()
-    g_f = [same(gs(yh, qm), dxp)]
-    pg.append(same(gs(yh, qm), partner))
-    g_a[1].wait_recv()
-    pg.append(same(gs(yh, qp), partner))
-
-    for m in m_hf + m_s3:
-        m.wait_recv()
-    for i in range(8):
-        mext[i * 64:(i + 1) * 64, 0:128] = halo[i, 0]
-        mext[i * 64:(i + 1) * 64, 2176:2304] = halo[i, 1]
-
+    m_ca = Group(ca.at[0:7])
+    m_ca.same(ca.at[f], *f_peers)
+
+    st_far.recv()
     for c in range(9):
         cols = slice(c * 256, (c + 1) * 256)
         r = dot(wg[0:576, :], mext[:, cols])
@@ -262,11 +257,6 @@
         w1m[:, cols] = r[192:384]
         ubuf[:, cols] = r[384:576].astype(BF)
 
-    g_b[0].wait_recv()
-    pg.append(same(gs(yo, qm), partner))
-    g_b[1].wait_recv()
-    g_f.append(same(gs(yo, qp), dxm))
-    pg.append(same(gs(yo, qp), partner))
     loc[1].wait()
 
     def diffuse(buf, t):
@@ -293,31 +283,58 @@
     first(0)
     first(15)
     tile = lambda i: vbuf.at[:, pl.ds(i * 128, 128)]
-    m_vh = [send(tile(1), tile(17), dleft), send(tile(16), tile(0), dright)]
+    m_vh = Group(vbuf.at[:, 0:256])
+    m_vh.send(tile(1), tile(17), dleft)
+    m_vh.send(tile(16), tile(0), dright)
     for t in range(1, 15):
         first(t)
-    g_f[0].wait_recv()
-    pg.append(same(gs(yh, q2), partner))
-    g_f[1].wait_recv()
-    pg.append(same(gs(yo, q2), partner))
+    m_ca.recv()
+    early = list(groups)
+    gall = (gall0, gall1, gall2)
+    slot = lambda g, a, b: gall[g].at[pl.ds(2 * (a * 8 + b), 2)]
+    yo = 1 - yh
+    several = lambda n: [Group(gall[g].at[0:2 * n]) for g in range(3)]
+    g_x, g_y, g_b, g_f, g_p = several(2), several(1), several(2), several(2), several(8)
+    for g in range(3):
+        r = dot(wg[576 + g * 64:640 + g * 64, :], ca[...].reshape(512, 256)).astype(BF)
+        gall[g][2 * d] = r[:, :128]
+        gall[g][2 * d + 1] = r[:, 128:]
+        g_y[g].same(slot(g, yh, q), yother)
+        g_x[g].same(slot(g, yh, q), dxp, dxm)
+        g_p[g].same(slot(g, yh, q), partner)
+
     for t in range(1, 15):
         second(t)
-    for m in m_vh:
-        m.wait_recv()
+    for g in range(3):
+        g_x[g].recv()
+        g_f[g].same(slot(g, yh, qm), dxp)
+        g_p[g].same(slot(g, yh, qm), partner)
+        g_p[g].same(slot(g, yh, qp), partner)
+
+    def pass_y(g):
+        g_y[g].recv()
+        g_b[g].same(slot(g, yo, q), dxp, dxm)
+        g_p[g].same(slot(g, yo, q), partner)
+
+    def pass_b(g):
+        g_b[g].recv()
+        g_f[g].same(slot(g, yo, qp), dxm)
+        g_p[g].same(slot(g, yo, qp), partner)
+        g_p[g].same(slot(g, yo, qm), partner)
+
+    def pass_f(g):
+        g_f[g].recv()
+        g_p[g].same(slot(g, yh, q2), partner)
+        g_p[g].same(slot(g, yo, q2), partner)
+
+    pass_y(0)
+    m_vh.recv()
     second(0)
     second(15)
-
-    for m in pg:
-        m.wait_recv()
+    pass_y(1)
+    for m in early:
+        m.sent()
     loc[2].wait()
-
-    for s in range(16):
-        parts = []
-        for t in (2 * s, 2 * s + 1):
-            lhs = jnp.concatenate([gall[ccols[k, t]] for k in range(2)], axis=1)
-            parts.append(gall[t].astype(F32) + dot(lhs, ct[t]))
-        gmix[s] = jnp.concatenate(parts, axis=1).astype(BF)
-
     eye = lax.broadcasted_iota(jnp.int32, (64, 64), 0) == lax.broadcasted_iota(
         jnp.int32, (64, 64), 1
     )
@@ -326,27 +343,52 @@
     win = [w_in[g].astype(F32) for g in range(3)]
     wcol = [[column(win[g][i:i + 1]) for i in range(2)] for g in range(3)]
 
-    for n in range(8):
-        cols = slice(n * 256, (n + 1) * 256)
-        ecols = slice(n * 256 + 128, (n + 1) * 256 + 128)
-        hi_n = cluster[:, cols] >> 8
-        oh = ohlo[:, cols]
-        acc = dot(gmix[0], oh)
-        for s in range(1, 16):
-            acc = jnp.where(hi_n == s, dot(gmix[s], oh), acc)
-        pre = acc + gsum[:, ecols]
-        xi = xin[:, cols].astype(F32)
-        terms = [wcol[g][0] * xi[0:1] + wcol[g][1] * xi[1:2] + bcol[g] for g in range(3)]
-        update = jax.nn.sigmoid(terms[0] + pre[0:64])
-        reset = jax.nn.sigmoid(terms[1] + pre[64:128])
-        cand = jnp.tanh(terms[2] + reset * pre[128:192])
-        mk = (lax.broadcasted_iota(jnp.int32, (1, 256), 1) + n * 256 < nvalid).astype(F32)
-        ms = state[:, cols].astype(F32) * mk
-        out[:, cols] = ((update * ms + (1.0 - update) * cand) * mk).astype(BF)
-
-    for m in msgs:
-        m.wait_send()
-    assert len(msgs) <= N_MSG
+    def unpool(g):
+        g_p[g].recv()
+        for s in range(16):
+            parts = []
+            for t in (2 * s, 2 * s + 1):
+                lhs = jnp.concatenate([gall[g][ccols[k, t]] for k in range(2)], axis=1)
+                parts.append(gall[g][t].astype(F32) + dot(lhs, ct[t]))
+            gmix[s] = jnp.concatenate(parts, axis=1).astype(BF)
+        if g < 2:
+            pass_f(g + 1)
+        rows = slice(g * 64, (g + 1) * 64)
+        for n in range(8):
+            cols = slice(n * 256, (n + 1) * 256)
+            ecols = slice(n * 256 + 128, (n + 1) * 256 + 128)
+            hi_n = cluster[:, cols] >> 8
+            r = dot(gmix[...].reshape(1024, 256), ohlo[:, cols])
+            acc = r[0:64]
+            for s in range(1, 16):
+                acc = jnp.where(hi_n == s, r[s * 64:(s + 1) * 64], acc)
+            pre = acc + gsum[rows, ecols]
+            xi = xin[:, cols].astype(F32)
+            terms = wcol[g][0] * xi[0:1] + wcol[g][1] * xi[1:2] + bcol[g]
+            if g < 2:
+                gsum[rows, ecols] = jax.nn.sigmoid(terms + pre)
+                continue
+            update, reset = gsum[0:64, ecols], gsum[64:128, ecols]
+            cand = jnp.tanh(terms + reset * pre)
+            mk = (lax.broadcasted_iota(jnp.int32, (1, 256), 1) + n * 256 < nvalid).astype(F32)
+            ms = state[:, cols].astype(F32) * mk
+            out[:, cols] = ((update * ms + (1.0 - update) * cand) * mk).astype(BF)
+            cp = pltpu.make_async_copy(out.at[:, cols], out_hbm.at[:, cols], lsem.at[23])
+            cp.start()
+
+    pass_b(0)
+    pass_y(2)
+    pass_b(1)
+    pass_f(0)
+    pass_b(2)
+    unpool(0)
+    unpool(1)
+    unpool(2)
+
+    for m in groups[len(early):]:
+        m.sent()
+    pltpu.make_async_copy(out, out_hbm, lsem.at[23]).wait()
+    assert len(groups) == N_MSG
 
 
 def body(
@@ -361,10 +403,9 @@
         kernel,
         out_shape=jax.ShapeDtypeStruct(state.shape, BF),
         in_specs=[vm, vm, hb, sm, sm, vm, hb, vm, vm, vm, hb, hb, hb, sm],
-        out_specs=vm,
+        out_specs=hb,
         scratch_shapes=[
             V((512, 2304), BF),
-            V((8, 2, 64, 128), BF),
             V((256, 2048), BF),
             V((80, 2048), F32),
             V((640, 2048), BF),
@@ -383,19 +424,22 @@
             V((8, 2, 64, 256), BF),
             V((2, 64, 256), F32),
             V((8, 64, 256), BF),
-            V((32, 192, 128), BF),
-            V((16, 192, 256), BF),
+            V((32, 64, 128), BF),
+            V((32, 64, 128), BF),
+            V((32, 64, 128), BF),
+            V((16, 64, 256), BF),
             V((192, 2304), BF),
             V((192, 2304), BF),
             V((192, 2304), F32),
             V((192, 2304), F32),
+            V((64, 2048), BF),
             V((16, 512, 128), BF),
             V((192, 4, 512), BF),
             V((768, 512), BF),
             V((32, 256, 128), BF),
             pltpu.SemaphoreType.DMA((N_MSG,)),
             pltpu.SemaphoreType.DMA((N_MSG,)),
-            pltpu.SemaphoreType.DMA((23,)),
+            pltpu.SemaphoreType.DMA((24,)),
         ],
         compiler_params=pltpu.CompilerParams(collective_id=0, has_side_effects=True),
     )(

time: 59.8 us -> 61.1 us (1.022)
  the two profiles are of different devices: /device:TPU:7 before, /device:TPU:1 now
where the time goes in v3:
time: 61.1 us; the launch traced here: 61 us
  Pallas kernels  58.7 us (96%)
  local copies, waits for them, and re-layouts  1.67 us (3%)
  between operations  0.66 us (1%)
    pallas_call x1, Pallas kernels, body(): pl.pallas_call(kernel, out_shape=jax.ShapeDtypeStruct(state.shape, BF), i...  58.7 us
    unnamed x1, local copies, waits for them, and re-layouts  1.67 us

profile of v3, /device:TPU:1, one launch (start us, length us, event | category | flops | bytes accessed | tf_op | source)
XLA Modules:
  0.0 61.0 jit_solution(9872006088644817773)
XLA Ops:
  0.7 58.7 %shard_map.136 = bf16[64,2048]{1,0:T(8,128)(2,1)} custom-call(bf16[64,2048]{1,0:T(8,128)(2,1)} %state.1, bf16[2,2048]{1,0:T(2,128)(2,1)} %xin.1, bf16[16,512,128]{2,1,0:T(8,128)(2,1)} %bitcast.10, s32[4,16]{1,0:T(4,128)} %bitcast.17, s32[1]{0:T(128)S(6)} %copy.16.valid, s32[1,2048]{1,0:T(1,128)} %bitcast.16, bf16[192,4,512]{2,1,0:T(4,128)(2,1)} %bitcast.12, ...), custom_call_target="tpu_custom_call" | custom-call | tf_op jit(solution)/shard_map/pallas_call | solution.py:402
  59.3 1.7 %copy.17 = bf16[64,2048]{1,0:T(8,128)(2,1)} copy(bf16[64,2048]{1,0:T(8,128)(2,1)} %shard_map.136) | data formatting | bytes 524288

commit v4 on v3

--- a/solution.py
+++ b/solution.py
@@ -8,7 +8,7 @@
 MESH = pl.DeviceIdType.MESH
 BF = jnp.bfloat16
 F32 = jnp.float32
-N_MSG = 28
+N_MSG = 21
 
 
 def dot(a, b, dims=((1,), (0,))):
@@ -23,33 +23,24 @@
     return a, b, c
 
 
-def split_counts(total):
-    high = jnp.floor(total * (1.0 / 256.0)) * 256.0
-    low = total - high
-    row = lax.broadcasted_iota(jnp.int32, (16, total.shape[1]), 0)
-    return jnp.where(row == 0, high, jnp.where(row == 1, low, 0.0))
-
-
 def kernel(
     state, xin, adj_hbm, adj_cols, valid, cluster, wg_hbm, w_in, bias, w_val, src_hbm, tgt_hbm,
     ct_hbm, ccols, out_hbm,
-    mext, ohlo, base, pl_lhs, pool, r1, s1, r2, s2, r3, src, tgt, t6, s6, scores, expo,
-    vals, pooled, ca, gall0, gall1, gall2, gmix, ubuf, vbuf, w1m, gsum, out, adj, wraw, wg, ct,
+    mext, ohlo, base, pl_lhs, pool, pcnt, r1, c1, s1, s1cnt, rs, rscnt, src, tgt, t6, s6, scores, expo,
+    vals, ca, gall0, gall1, gall2, gmix, ubuf, vbuf, w1m, gsum, out, adj, wraw, wg, ct,
     ssem, rsem, lsem,
 ):
     d = lax.axis_index("dom")
     f = lax.axis_index("feat")
     core, x, yh = d % 2, (d // 2) % 4, d // 8
     z, yl = f // 2, f % 2
-    xp, xm, x2 = (x + 1) % 4, (x + 3) % 4, (x + 2) % 4
     zp, zm = (z + 1) % 4, (z + 3) % 4
-    q, qp, qm, q2 = (i * 2 + core for i in (x, xp, xm, x2))
     dev = lambda i: (i, f)
     fdev = lambda i: (d, i)
-    partner, yother = dev(d + 1 - 2 * core), dev((d + 8) % 16)
-    dxp, dxm, dx2 = (dev(yh * 8 + i) for i in (qp, qm, q2))
-    rq, rqp, rqm, rq2 = (i * 2 + 1 - core for i in (x, xp, xm, x2))
-    pxp, pxm = (dev(yh * 8 + i) for i in (rqp, rqm))
+    partner = dev(d + 1 - 2 * core)
+    hops = [(2, 1), (1, 1), (3, 1), (2, 0), (0, 1), (1, 0), (3, 0)]
+    chip = lambda a, b: ((yh + b) % 2) * 8 + ((x + a) % 4) * 2
+    chips = [dev(chip(a, b) + core) for a, b in hops]
     dleft, dright = dev((d + 15) % 16), dev((d + 1) % 16)
     fi = lambda a, b: a * 2 + b
     fy, fzp, fzm = f + 1 - 2 * yl, fi(zp, yl), fi(zm, yl)
@@ -98,7 +89,7 @@
 
     barrier = pltpu.get_barrier_semaphore()
     cross = dev((d + 15 + 2 * core) % 16)
-    peers = [partner, cross, yother, dxp, dxm, dx2, pxp, pxm] + f_peers
+    peers = [partner, cross] + chips + f_peers
     for p in peers:
         pl.semaphore_signal(barrier, inc=1, device_id=p, device_id_type=MESH)
 
@@ -108,37 +99,45 @@
     myrows = pl.ds(pl.multiple_of(f * 64, 64), 64)
     own = pl.ds(128, 2048)
     mext[myrows, own] = masked32.astype(BF)
-    base[0:64, :] = masked32
+    base[...] = masked32
     row16 = lax.broadcasted_iota(jnp.int32, (16, 2048), 0)
-    base[64:80, :] = jnp.where(row16 == 0, mask, 0.0)
     low = cluster[...] & 255
     high = cluster[...] >> 8
     ohlo[...] = (lax.broadcasted_iota(jnp.int32, (256, 2048), 0) == low).astype(F32).astype(BF)
+
+    row8 = lax.broadcasted_iota(jnp.int32, (8, 2048), 0)
+    row_high = (row8 & 1) * 8 + (row8 >> 1) * 2
 
     def pool_part(c, to_core):
         for xx in range(4):
             for yy in range(2):
                 slot = xx * 2 + yy
                 hit = high == (yy * 8 + xx * 2) + to_core
-                pl_lhs[slot * 80:(slot + 1) * 80, :] = jnp.where(hit, base[...], 0.0).astype(BF)
+                pl_lhs[slot * 64:(slot + 1) * 64, :] = jnp.where(hit, base[...], 0.0).astype(BF)
         for i in range(2):
-            res = dot(pl_lhs[i * 320:(i + 1) * 320, :], ohlo[...], ((1,), (1,)))
+            res = dot(pl_lhs[i * 256:(i + 1) * 256, :], ohlo[...], ((1,), (1,))).astype(BF)
             for k in range(4):
                 slot = i * 4 + k
-                r = res[k * 80:(k + 1) * 80]
-                pool[c, slot // 2, slot % 2] = jnp.concatenate(
-                    [r[:64], split_counts(r[64:65])], axis=0
-                ).astype(BF)
+                pool[c, slot // 2, slot % 2] = res[k * 64:(k + 1) * 64]
+        lhs = jnp.where(high == row_high + to_core, mask, 0.0).astype(BF)
+        pcnt[c] = dot(lhs, ohlo[...], ((1,), (1,)))
 
     pool_part(0, 1 - core)
 
     pl.semaphore_wait(barrier, len(peers))
 
-    m_r1 = Group(r1)
+    m_r1, m_c1 = Group(r1), Group(c1)
     m_r1.send(pool.at[0], r1, partner)
+    m_c1.send(pcnt.at[0], c1, partner)
+    mrow = lambda i, cols: mext.at[pl.ds(pl.multiple_of(i * 64, 64), 64), cols]
+    mhalf = lambda i, h: mext.at[pl.ds(pl.multiple_of(i * 64 + h * 32, 32), 32), :]
+    all_cols, left, right = pl.ds(0, 2304), pl.ds(0, 128), pl.ds(2176, 128)
     m_h = Group(mext.at[0:64, 0:256])
-    m_h.send(mext.at[myrows, pl.ds(128, 128)], mext.at[myrows, pl.ds(2176, 128)], dleft)
-    m_h.send(mext.at[myrows, pl.ds(2048, 128)], mext.at[myrows, pl.ds(0, 128)], dright)
+    m_h.send(mrow(f, pl.ds(128, 128)), mrow(f, right), dleft)
+    m_h.send(mrow(f, pl.ds(2048, 128)), mrow(f, left), dright)
+    st_y, st_z = Group(mext.at[0:64]), Group(mext.at[0:128])
+    st_y.same(mrow(f, own), fdev(fy))
+    st_z.same(mrow(f, own), fdev(fzp), fdev(fzm))
     pool_part(1, core)
 
     for c in emb:
@@ -157,31 +156,21 @@
         scores[cols, :] = s
         return jnp.maximum(peak, jnp.max(s.reshape(64, 8, 256), axis=0))
 
-    def add_blocks(blocks):
-        total = blocks[0][...].astype(F32)
-        for b in blocks[1:]:
-            total = total + b[...].astype(F32)
-        return total[:64], total[64:65] + total[65:66]
-
-    def packed(sums, cnt):
-        return jnp.concatenate([sums, split_counts(cnt)], axis=0).astype(BF)
-
     m_r1.recv()
-    for xx in range(4):
-        for yy in range(2):
-            s1[xx, yy] = packed(*add_blocks([pool.at[1, xx, yy], r1.at[xx, yy]]))
-    m_r2 = Group(r2)
-    m_r2.send(s1.at[x2], r2.at[2], dx2)
-    m_r2.send(s1.at[xp], r2.at[0], dxp)
-    m_r2.send(s1.at[xm], r2.at[1], dxm)
+    m_c1.recv()
+    s1[...] = (pool[1].astype(F32) + r1[...].astype(F32)).astype(BF)
+    s1cnt[...] = pcnt[1] + c1[...]
+    m_rs, m_rc = Group(rs.at[0:7]), Group(rscnt.at[0:7])
+    for k, (a, b) in enumerate(hops):
+        xx, yy = (x + a) % 4, (yh + b) % 2
+        m_rs.send(s1.at[xx, yy], rs.at[k], chips[k])
+        m_rc.send(s1cnt.at[pl.ds(xx * 2 + yy, 1)], rscnt.at[k], chips[k])
 
     peak = lax.fori_loop(0, 4, score_step, jnp.zeros((8, 256), F32))
     m_h.recv()
-    mrow = lambda i: mext.at[pl.ds(pl.multiple_of(i * 64, 64), 64), :]
-    mhalf = lambda i, h: mext.at[pl.ds(pl.multiple_of(i * 64 + h * 32, 32), 32), :]
-    st_y, st_z = Group(mext.at[0:64]), Group(mext.at[0:128])
-    st_y.same(mrow(f), fdev(fy))
-    st_z.same(mrow(f), fdev(fzp), fdev(fzm))
+    for cols in (left, right):
+        st_y.same(mrow(f, cols), fdev(fy))
+        st_z.same(mrow(f, cols), fdev(fzp), fdev(fzm))
     peak = lax.fori_loop(4, 8, score_step, peak)
     peak = jnp.max(peak, axis=0, keepdims=True)
 
@@ -194,60 +183,59 @@
     total = lax.fori_loop(0, 8, exp_step, jnp.zeros((8, 256), F32))
     inv = 1.0 / jnp.sum(total, axis=0, keepdims=True)
 
-    m_r2.recv()
-    for yy in range(2):
-        s2[yy] = packed(*add_blocks([s1.at[x, yy]] + [r2.at[k, yy] for k in range(3)]))
-    m_r3 = Group(s2)
-    m_r3.send(s2, r3, yother)
-
     st_y.recv()
     st_yz = Group(mext.at[0:128])
-    st_yz.same(mrow(fy), fdev(fzp), fdev(fzm))
-    loc[0].wait()
-    for k in range(4):
-        wg[k * 192:(k + 1) * 192, :] = wraw[:, k, :]
-    m_r3.recv()
-    wv = w_val[...]
-    for yy in range(2):
-        sums, cnt = add_blocks([s2.at[yy], r3.at[yy]])
-        avg = sums / jnp.maximum(cnt, 1.0)
-        pooled[yy] = avg
-        pa, pb, pc = split3(avg)
-        vals[q, yy] = (dot(wv, pa) + dot(wv, pb) + dot(wv, pc)).astype(BF)
-
-    m_v, m_pv = Group(vals.at[0:2]), Group(vals.at[0:3])
-    m_v.same(vals.at[q], dxp, dxm)
-    m_pv.same(vals.at[q], partner)
-
-    def attend(total, i, halves=(0, 1)):
-        for yy in halves:
-            rows = pl.ds(pl.multiple_of((yy * 8 + i) * 256, 256), 256)
-            total = total + dot(vals[i, yy], expo[rows, :])
-        return total
-
-    att = attend(jnp.zeros((64, 256), F32), q)
+    st_yz.same(mrow(fy, all_cols), fdev(fzp), fdev(fzm))
     st_z.recv()
     st_far = Group(mext.at[0:128])
     st_far.same(mhalf(fzm, 0), fdev(fzp))
     st_far.same(mhalf(fzp, 1), fdev(fzm))
-    m_v.recv()
-    m_far = Group(vals.at[0:2])
-    m_far.same(vals.at[qm, 0], dxp, pxp)
-    m_far.same(vals.at[qp, 1], dxm, pxm)
-    m_pv.same(vals.at[qm], partner)
-    m_pv.same(vals.at[qp], partner)
-    att = attend(attend(att, qm), qp)
-    m_pv.recv()
-    for i in (rq, rqm, rqp):
-        att = attend(att, i)
+    m_rs.recv()
+    m_rc.recv()
+    sums, cnt = s1[x, yh].astype(F32), s1cnt[pl.ds(x * 2 + yh, 1), :]
+    for k in range(7):
+        sums = sums + rs[k].astype(F32)
+        cnt = cnt + rscnt[k]
+    pooled = sums / jnp.maximum(cnt, 1.0)
+    pa, pb, pc = split3(pooled)
+    wv = w_val[...]
+    vals[d] = (dot(wv, pa) + dot(wv, pb) + dot(wv, pc)).astype(BF)
+
+    near, far = Group(vals.at[0:4]), Group(vals.at[0:3])
+    for k in range(7):
+        (far if k < 3 else near).same(vals.at[d], chips[k])
+    swap_near, swap_far = Group(vals.at[0:5]), Group(vals.at[0:3])
+    swap_near.same(vals.at[d], partner)
+
+    loc[0].wait()
+    for k in range(4):
+        wg[k * 192:(k + 1) * 192, :] = wraw[:, k, :]
+
+    def attend(total, slots):
+        for i in slots:
+            rows = pl.ds(pl.multiple_of(i * 256, 256), 256)
+            total = total + dot(vals[i], expo[rows, :])
+        return total
+
+    mine_of = lambda ks, c: [chip(*hops[k]) + c for k in ks]
+    near.recv()
+    for i in mine_of(range(3, 7), core):
+        swap_near.same(vals.at[i], partner)
+    att = attend(jnp.zeros((64, 256), F32), [d] + mine_of(range(3, 7), core))
+    far.recv()
+    for i in mine_of(range(3), core):
+        swap_far.same(vals.at[i], partner)
+    swap_near.recv()
+    att = attend(att, mine_of(range(3), core) + [chip(0, 0) + 1 - core])
+    att = attend(att, mine_of(range(3, 7), 1 - core))
     st_yz.recv()
+    swap_far.recv()
+    att = attend(att, mine_of(range(3), 1 - core))
+    ca[f] = (pooled + att * inv).astype(BF)
+    m_ca = Group(ca.at[0:7])
+    m_ca.same(ca.at[f], *f_peers)
     st_far.same(mhalf(fi(zm, 1 - yl), 0), fdev(fzp))
     st_far.same(mhalf(fi(zp, 1 - yl), 1), fdev(fzm))
-    m_far.recv()
-    att = attend(attend(att, q2), rq2)
-    ca[f] = (pooled[yh] + att * inv).astype(BF)
-    m_ca = Group(ca.at[0:7])
-    m_ca.same(ca.at[f], *f_peers)
 
     st_far.recv()
     for c in range(9):
@@ -291,47 +279,26 @@
     m_ca.recv()
     early = list(groups)
     gall = (gall0, gall1, gall2)
-    slot = lambda g, a, b: gall[g].at[pl.ds(2 * (a * 8 + b), 2)]
-    yo = 1 - yh
+    slot = lambda g, i: gall[g].at[pl.ds(2 * i, 2)]
     several = lambda n: [Group(gall[g].at[0:2 * n]) for g in range(3)]
-    g_x, g_y, g_b, g_f, g_p = several(2), several(1), several(2), several(2), several(8)
+    g_x, g_p = several(7), several(8)
     for g in range(3):
         r = dot(wg[576 + g * 64:640 + g * 64, :], ca[...].reshape(512, 256)).astype(BF)
         gall[g][2 * d] = r[:, :128]
         gall[g][2 * d + 1] = r[:, 128:]
-        g_y[g].same(slot(g, yh, q), yother)
-        g_x[g].same(slot(g, yh, q), dxp, dxm)
-        g_p[g].same(slot(g, yh, q), partner)
+        g_x[g].same(slot(g, d), *chips)
+        g_p[g].same(slot(g, d), partner)
 
     for t in range(1, 15):
         second(t)
-    for g in range(3):
+    def swap(g):
         g_x[g].recv()
-        g_f[g].same(slot(g, yh, qm), dxp)
-        g_p[g].same(slot(g, yh, qm), partner)
-        g_p[g].same(slot(g, yh, qp), partner)
-
-    def pass_y(g):
-        g_y[g].recv()
-        g_b[g].same(slot(g, yo, q), dxp, dxm)
-        g_p[g].same(slot(g, yo, q), partner)
-
-    def pass_b(g):
-        g_b[g].recv()
-        g_f[g].same(slot(g, yo, qp), dxm)
-        g_p[g].same(slot(g, yo, qp), partner)
-        g_p[g].same(slot(g, yo, qm), partner)
-
-    def pass_f(g):
-        g_f[g].recv()
-        g_p[g].same(slot(g, yh, q2), partner)
-        g_p[g].same(slot(g, yo, q2), partner)
-
-    pass_y(0)
+        for i in mine_of(range(7), core):
+            g_p[g].same(slot(g, i), partner)
+
     m_vh.recv()
     second(0)
     second(15)
-    pass_y(1)
     for m in early:
         m.sent()
     loc[2].wait()
@@ -352,7 +319,7 @@
                 parts.append(gall[g][t].astype(F32) + dot(lhs, ct[t]))
             gmix[s] = jnp.concatenate(parts, axis=1).astype(BF)
         if g < 2:
-            pass_f(g + 1)
+            swap(g + 1)
         rows = slice(g * 64, (g + 1) * 64)
         for n in range(8):
             cols = slice(n * 256, (n + 1) * 256)
@@ -376,11 +343,7 @@
             cp = pltpu.make_async_copy(out.at[:, cols], out_hbm.at[:, cols], lsem.at[23])
             cp.start()
 
-    pass_b(0)
-    pass_y(2)
-    pass_b(1)
-    pass_f(0)
-    pass_b(2)
+    swap(0)
     unpool(0)
     unpool(1)
     unpool(2)
@@ -407,22 +370,23 @@
         scratch_shapes=[
             V((512, 2304), BF),
             V((256, 2048), BF),
-            V((80, 2048), F32),
-            V((640, 2048), BF),
-            V((2, 4, 2, 80, 256), BF),
-            V((4, 2, 80, 256), BF),
-            V((4, 2, 80, 256), BF),
-            V((3, 2, 80, 256), BF),
-            V((2, 80, 256), BF),
-            V((2, 80, 256), BF),
+            V((64, 2048), F32),
+            V((512, 2048), BF),
+            V((2, 4, 2, 64, 256), BF),
+            V((2, 8, 256), F32),
+            V((4, 2, 64, 256), BF),
+            V((8, 256), F32),
+            V((4, 2, 64, 256), BF),
+            V((8, 256), F32),
+            V((7, 64, 256), BF),
+            V((7, 1, 256), F32),
             V((16, 256), F32),
             V((16, 4096), F32),
             V((96, 4096), BF),
             V((96, 256), BF),
             V((4096, 256), F32),
             V((4096, 256), BF),
-            V((8, 2, 64, 256), BF),
-            V((2, 64, 256), F32),
+            V((16, 64, 256), BF),
             V((8, 64, 256), BF),
             V((32, 64, 128), BF),
             V((32, 64, 128), BF),

time: 61.1 us -> 58.8 us (0.962)
  Pallas kernels: 58.7 us -> 56.3 us
    pallas_call x1, Pallas kernels: 58.7 us -> 56.3 us  [body(): pl.pallas_call(kernel, out_shape=jax.ShapeDtypeStruct(state.shape, BF), i...]
where the time goes in v4:
time: 58.8 us; the launch traced here: 58.7 us
  Pallas kernels  56.3 us (96%)
  local copies, waits for them, and re-layouts  1.67 us (3%)
  between operations  0.66 us (1%)
    pallas_call x1, Pallas kernels, body(): pl.pallas_call(kernel, out_shape=jax.ShapeDtypeStruct(state.shape, BF), i...  56.3 us
    unnamed x1, local copies, waits for them, and re-layouts  1.67 us

profile of v4, /device:TPU:1, one launch (start us, length us, event | category | flops | bytes accessed | tf_op | source)
XLA Modules:
  0.0 58.7 jit_solution(6678897814754685787)
XLA Ops:
  0.7 56.3 %shard_map.136 = bf16[64,2048]{1,0:T(8,128)(2,1)} custom-call(bf16[64,2048]{1,0:T(8,128)(2,1)} %state.1, bf16[2,2048]{1,0:T(2,128)(2,1)} %xin.1, bf16[16,512,128]{2,1,0:T(8,128)(2,1)} %bitcast.10, s32[4,16]{1,0:T(4,128)} %bitcast.17, s32[1]{0:T(128)S(6)} %copy.16.valid, s32[1,2048]{1,0:T(1,128)} %bitcast.16, bf16[192,4,512]{2,1,0:T(4,128)(2,1)} %bitcast.12, ...), custom_call_target="tpu_custom_call" | custom-call | tf_op jit(solution)/shard_map/pallas_call | solution.py:365
  57.0 1.7 %copy.17 = bf16[64,2048]{1,0:T(8,128)(2,1)} copy(bf16[64,2048]{1,0:T(8,128)(2,1)} %shard_map.136) | data formatting | bytes 524288

commit v5 on v4

--- a/solution.py
+++ b/solution.py
@@ -8,7 +8,7 @@
 MESH = pl.DeviceIdType.MESH
 BF = jnp.bfloat16
 F32 = jnp.float32
-N_MSG = 21
+N_MSG = 24
 
 
 def dot(a, b, dims=((1,), (0,))):
@@ -26,7 +26,7 @@
 def kernel(
     state, xin, adj_hbm, adj_cols, valid, cluster, wg_hbm, w_in, bias, w_val, src_hbm, tgt_hbm,
     ct_hbm, ccols, out_hbm,
-    mext, ohlo, base, pl_lhs, pool, pcnt, r1, c1, s1, s1cnt, rs, rscnt, src, tgt, t6, s6, scores, expo,
+    mext, halo, ohlo, base, pl_lhs, pool, pcnt, r1, c1, s1, s1cnt, rs, rscnt, src, tgt, t6, s6, scores, expo,
     vals, ca, gall0, gall1, gall2, gmix, ubuf, vbuf, w1m, gsum, out, adj, wraw, wg, ct,
     ssem, rsem, lsem,
 ):
@@ -129,15 +129,16 @@
     m_r1, m_c1 = Group(r1), Group(c1)
     m_r1.send(pool.at[0], r1, partner)
     m_c1.send(pcnt.at[0], c1, partner)
-    mrow = lambda i, cols: mext.at[pl.ds(pl.multiple_of(i * 64, 64), 64), cols]
-    mhalf = lambda i, h: mext.at[pl.ds(pl.multiple_of(i * 64 + h * 32, 32), 32), :]
-    all_cols, left, right = pl.ds(0, 2304), pl.ds(0, 128), pl.ds(2176, 128)
-    m_h = Group(mext.at[0:64, 0:256])
-    m_h.send(mrow(f, pl.ds(128, 128)), mrow(f, right), dleft)
-    m_h.send(mrow(f, pl.ds(2048, 128)), mrow(f, left), dright)
-    st_y, st_z = Group(mext.at[0:64]), Group(mext.at[0:128])
-    st_y.same(mrow(f, own), fdev(fy))
-    st_z.same(mrow(f, own), fdev(fzp), fdev(fzm))
+    mrow = lambda i: mext.at[pl.ds(pl.multiple_of(i * 64, 64), 64), own]
+    mhalf = lambda i, h: mext.at[pl.ds(pl.multiple_of(i * 64 + h * 32, 32), 32), own]
+    st_y = [Group(mext.at[0:32, own]) for h in range(2)]
+    st_yz = [Group(mext.at[0:64, own]) for h in range(2)]
+    st_z, st_far = Group(mext.at[0:128, own]), Group(mext.at[0:128, own])
+    m_h = Group(halo.at[0])
+    m_h.send(mext.at[myrows, pl.ds(128, 128)], halo.at[f, 1], dleft)
+    m_h.send(mext.at[myrows, pl.ds(2048, 128)], halo.at[f, 0], dright)
+    st_y[0].same(mhalf(f, 0), fdev(fy))
+    st_z.same(mrow(f), fdev(fzp), fdev(fzm))
     pool_part(1, core)
 
     for c in emb:
@@ -166,11 +167,8 @@
         m_rs.send(s1.at[xx, yy], rs.at[k], chips[k])
         m_rc.send(s1cnt.at[pl.ds(xx * 2 + yy, 1)], rscnt.at[k], chips[k])
 
+    st_y[1].same(mhalf(f, 1), fdev(fy))
     peak = lax.fori_loop(0, 4, score_step, jnp.zeros((8, 256), F32))
-    m_h.recv()
-    for cols in (left, right):
-        st_y.same(mrow(f, cols), fdev(fy))
-        st_z.same(mrow(f, cols), fdev(fzp), fdev(fzm))
     peak = lax.fori_loop(4, 8, score_step, peak)
     peak = jnp.max(peak, axis=0, keepdims=True)
 
@@ -183,13 +181,14 @@
     total = lax.fori_loop(0, 8, exp_step, jnp.zeros((8, 256), F32))
     inv = 1.0 / jnp.sum(total, axis=0, keepdims=True)
 
-    st_y.recv()
-    st_yz = Group(mext.at[0:128])
-    st_yz.same(mrow(fy, all_cols), fdev(fzp), fdev(fzm))
+    st_y[0].recv()
+    st_yz[0].same(mhalf(fy, 0), fdev(fzp), fdev(fzm))
     st_z.recv()
-    st_far = Group(mext.at[0:128])
     st_far.same(mhalf(fzm, 0), fdev(fzp))
     st_far.same(mhalf(fzp, 1), fdev(fzm))
+    m_h.recv()
+    m_hs = Group(halo.at[0:7])
+    m_hs.same(halo.at[f], *f_peers)
     m_rs.recv()
     m_rc.recv()
     sums, cnt = s1[x, yh].astype(F32), s1cnt[pl.ds(x * 2 + yh, 1), :]
@@ -207,6 +206,8 @@
     swap_near, swap_far = Group(vals.at[0:5]), Group(vals.at[0:3])
     swap_near.same(vals.at[d], partner)
 
+    st_y[1].recv()
+    st_yz[1].same(mhalf(fy, 1), fdev(fzp), fdev(fzm))
     loc[0].wait()
     for k in range(4):
         wg[k * 192:(k + 1) * 192, :] = wraw[:, k, :]
@@ -217,6 +218,8 @@
             total = total + dot(vals[i], expo[rows, :])
         return total
 
+    st_yz[0].recv()
+    st_far.same(mhalf(fi(zm, 1 - yl), 0), fdev(fzp))
     mine_of = lambda ks, c: [chip(*hops[k]) + c for k in ks]
     near.recv()
     for i in mine_of(range(3, 7), core):
@@ -228,54 +231,13 @@
     swap_near.recv()
     att = attend(att, mine_of(range(3), core) + [chip(0, 0) + 1 - core])
     att = attend(att, mine_of(range(3, 7), 1 - core))
-    st_yz.recv()
     swap_far.recv()
     att = attend(att, mine_of(range(3), 1 - core))
     ca[f] = (pooled + att * inv).astype(BF)
     m_ca = Group(ca.at[0:7])
     m_ca.same(ca.at[f], *f_peers)
-    st_far.same(mhalf(fi(zm, 1 - yl), 0), fdev(fzp))
+    st_yz[1].recv()
     st_far.same(mhalf(fi(zp, 1 - yl), 1), fdev(fzm))
-
-    st_far.recv()
-    for c in range(9):
-        cols = slice(c * 256, (c + 1) * 256)
-        r = dot(wg[0:576, :], mext[:, cols])
-        gsum[:, cols] = r[0:192]
-        w1m[:, cols] = r[192:384]
-        ubuf[:, cols] = r[384:576].astype(BF)
-
-    loc[1].wait()
-
-    def diffuse(buf, t):
-        lo, mid, hi = (buf[:, (t + k) * 128:(t + k + 1) * 128] for k in range(3))
-
-        def pick(k):
-            c = jnp.full((1, 128), adj_cols[k, t], jnp.int32)
-            wlo, wmid, whi = ((c == t + i).astype(F32).astype(BF) for i in range(3))
-            return lo * wlo + mid * wmid + hi * whi
-
-        lhs = jnp.concatenate([lo, pick(1), pick(2), hi], axis=1)
-        r = dot(lhs, adj[t])
-        pos = lax.broadcasted_iota(jnp.int32, (1, 128), 1) + t * 128
-        return r * (pos < nvalid).astype(F32)
-
-    def first(t):
-        cols = slice((t + 1) * 128, (t + 2) * 128)
-        vbuf[:, cols] = (w1m[:, cols] + diffuse(ubuf, t)).astype(BF)
-
-    def second(t):
-        cols = slice((t + 1) * 128, (t + 2) * 128)
-        gsum[:, cols] = gsum[:, cols] + diffuse(vbuf, t)
-
-    first(0)
-    first(15)
-    tile = lambda i: vbuf.at[:, pl.ds(i * 128, 128)]
-    m_vh = Group(vbuf.at[:, 0:256])
-    m_vh.send(tile(1), tile(17), dleft)
-    m_vh.send(tile(16), tile(0), dright)
-    for t in range(1, 15):
-        first(t)
     m_ca.recv()
     early = list(groups)
     gall = (gall0, gall1, gall2)
@@ -289,6 +251,50 @@
         g_x[g].same(slot(g, d), *chips)
         g_p[g].same(slot(g, d), partner)
 
+    st_far.recv()
+    m_hs.recv()
+    for i in range(8):
+        mext[i * 64:(i + 1) * 64, 0:128] = halo[i, 0]
+        mext[i * 64:(i + 1) * 64, 2176:2304] = halo[i, 1]
+
+    for c in range(9):
+        cols = slice(c * 256, (c + 1) * 256)
+        r = dot(wg[0:576, :], mext[:, cols])
+        gsum[:, cols] = r[0:192]
+        w1m[:, cols] = r[192:384]
+        ubuf[:, cols] = r[384:576].astype(BF)
+
+    loc[1].wait()
+
+    def diffuse(buf, t):
+        lo, mid, hi = (buf[:, (t + k) * 128:(t + k + 1) * 128] for k in range(3))
+
+        def pick(k):
+            c = jnp.full((1, 128), adj_cols[k, t], jnp.int32)
+            wlo, wmid, whi = ((c == t + i).astype(F32).astype(BF) for i in range(3))
+            return lo * wlo + mid * wmid + hi * whi
+
+        lhs = jnp.concatenate([lo, pick(1), pick(2), hi], axis=1)
+        r = dot(lhs, adj[t])
+        pos = lax.broadcasted_iota(jnp.int32, (1, 128), 1) + t * 128
+        return r * (pos < nvalid).astype(F32)
+
+    def first(t):
+        cols = slice((t + 1) * 128, (t + 2) * 128)
+        vbuf[:, cols] = (w1m[:, cols] + diffuse(ubuf, t)).astype(BF)
+
+    def second(t):
+        cols = slice((t + 1) * 128, (t + 2) * 128)
+        gsum[:, cols] = gsum[:, cols] + diffuse(vbuf, t)
+
+    first(0)
+    first(15)
+    tile = lambda i: vbuf.at[:, pl.ds(i * 128, 128)]
+    m_vh = Group(vbuf.at[:, 0:256])
+    m_vh.send(tile(1), tile(17), dleft)
+    m_vh.send(tile(16), tile(0), dright)
+    for t in range(1, 15):
+        first(t)
     for t in range(1, 15):
         second(t)
     def swap(g):
@@ -296,9 +302,6 @@
         for i in mine_of(range(7), core):
             g_p[g].same(slot(g, i), partner)
 
-    m_vh.recv()
-    second(0)
-    second(15)
     for m in early:
         m.sent()
     loc[2].wait()
@@ -332,7 +335,11 @@
             pre = acc + gsum[rows, ecols]
             xi = xin[:, cols].astype(F32)
             terms = wcol[g][0] * xi[0:1] + wcol[g][1] * xi[1:2] + bcol[g]
-            if g < 2:
+            if g == 0:
+                gsum[rows, ecols] = terms + pre
+                continue
+            if g == 1:
+                gsum[0:64, ecols] = jax.nn.sigmoid(gsum[0:64, ecols])
                 gsum[rows, ecols] = jax.nn.sigmoid(terms + pre)
                 continue
             update, reset = gsum[0:64, ecols], gsum[64:128, ecols]
@@ -345,6 +352,9 @@
 
     swap(0)
     unpool(0)
+    m_vh.recv()
+    second(0)
+    second(15)
     unpool(1)
     unpool(2)
 
@@ -369,6 +379,7 @@
         out_specs=hb,
         scratch_shapes=[
             V((512, 2304), BF),
+            V((8, 2, 64, 128), BF),
             V((256, 2048), BF),
             V((64, 2048), F32),
             V((512, 2048), BF),

time: 58.8 us -> 53.6 us (0.912)
  Pallas kernels: 56.3 us -> 51.1 us
    pallas_call x1, Pallas kernels: 56.3 us -> 51.1 us  [body(): pl.pallas_call(kernel, out_shape=jax.ShapeDtypeStruct(state.shape, BF), i...]
where the time goes in v5:
time: 53.6 us; the launch traced here: 53.4 us
  Pallas kernels  51.1 us (95%)
  local copies, waits for them, and re-layouts  1.67 us (3%)
  between operations  0.66 us (1%)
    pallas_call x1, Pallas kernels, body(): pl.pallas_call(kernel, out_shape=jax.ShapeDtypeStruct(state.shape, BF), i...  51.1 us
    unnamed x1, local copies, waits for them, and re-layouts  1.67 us

profile of v5, /device:TPU:1, one launch (start us, length us, event | category | flops | bytes accessed | tf_op | source)
XLA Modules:
  0.0 53.4 jit_solution(17868086456513052234)
XLA Ops:
  0.7 51.1 %shard_map.136 = bf16[64,2048]{1,0:T(8,128)(2,1)} custom-call(bf16[64,2048]{1,0:T(8,128)(2,1)} %state.1, bf16[2,2048]{1,0:T(2,128)(2,1)} %xin.1, bf16[16,512,128]{2,1,0:T(8,128)(2,1)} %bitcast.10, s32[4,16]{1,0:T(4,128)} %bitcast.17, s32[1]{0:T(128)S(6)} %copy.16.valid, s32[1,2048]{1,0:T(1,128)} %bitcast.16, bf16[192,4,512]{2,1,0:T(4,128)(2,1)} %bitcast.12, ...), custom_call_target="tpu_custom_call" | custom-call | tf_op jit(solution)/shard_map/pallas_call | solution.py:375
  51.7 1.7 %copy.17 = bf16[64,2048]{1,0:T(8,128)(2,1)} copy(bf16[64,2048]{1,0:T(8,128)(2,1)} %shard_map.136) | data formatting | bytes 524288

commit v6 on v5

--- a/solution.py
+++ b/solution.py
@@ -8,7 +8,7 @@
 MESH = pl.DeviceIdType.MESH
 BF = jnp.bfloat16
 F32 = jnp.float32
-N_MSG = 24
+N_MSG = 25
 
 
 def dot(a, b, dims=((1,), (0,))):
@@ -27,7 +27,7 @@
     state, xin, adj_hbm, adj_cols, valid, cluster, wg_hbm, w_in, bias, w_val, src_hbm, tgt_hbm,
     ct_hbm, ccols, out_hbm,
     mext, halo, ohlo, base, pl_lhs, pool, pcnt, r1, c1, s1, s1cnt, rs, rscnt, src, tgt, t6, s6, scores, expo,
-    vals, ca, gall0, gall1, gall2, gmix, ubuf, vbuf, w1m, gsum, out, adj, wraw, wg, ct,
+    vals, ca, gall0, gall1, gall2, gall3, gmix, gmix_half, ubuf, vbuf, w1m, gsum, out, adj, wraw, wg, ct,
     ssem, rsem, lsem,
 ):
     d = lax.axis_index("dom")
@@ -78,13 +78,9 @@
         pltpu.make_async_copy(adj_hbm, adj, lsem.at[1]),
         pltpu.make_async_copy(ct_hbm, ct, lsem.at[2]),
     ]
-    emb = []
-    for r in range(10):
-        emb.append(pltpu.make_async_copy(tgt_hbm.at[r], tgt.at[pl.ds(r, 1)], lsem.at[3 + r]))
-        emb.append(
-            pltpu.make_async_copy(src_hbm.at[r, :, mine], src.at[pl.ds(r, 1)], lsem.at[13 + r])
-        )
-    for c in emb + loc:
+    tgt_rows = [pltpu.make_async_copy(tgt_hbm.at[r], tgt.at[pl.ds(r, 1)], lsem.at[3]) for r in range(10)]
+    src_rows = pltpu.make_async_copy(src_hbm.at[:, :, mine], src, lsem.at[4])
+    for c in tgt_rows + [src_rows] + loc:
         c.start()
 
     barrier = pltpu.get_barrier_semaphore()
@@ -98,9 +94,8 @@
     masked32 = state[...].astype(F32) * mask
     myrows = pl.ds(pl.multiple_of(f * 64, 64), 64)
     own = pl.ds(128, 2048)
-    mext[myrows, own] = masked32.astype(BF)
-    base[...] = masked32
-    row16 = lax.broadcasted_iota(jnp.int32, (16, 2048), 0)
+    base[...] = masked32.astype(BF)
+    mext[myrows, own] = base[...]
     low = cluster[...] & 255
     high = cluster[...] >> 8
     ohlo[...] = (lax.broadcasted_iota(jnp.int32, (256, 2048), 0) == low).astype(F32).astype(BF)
@@ -113,7 +108,7 @@
             for yy in range(2):
                 slot = xx * 2 + yy
                 hit = high == (yy * 8 + xx * 2) + to_core
-                pl_lhs[slot * 64:(slot + 1) * 64, :] = jnp.where(hit, base[...], 0.0).astype(BF)
+                pl_lhs[slot * 64:(slot + 1) * 64, :] = base[...] * hit.astype(F32).astype(BF)
         for i in range(2):
             res = dot(pl_lhs[i * 256:(i + 1) * 256, :], ohlo[...], ((1,), (1,))).astype(BF)
             for k in range(4):
@@ -131,9 +126,9 @@
     m_c1.send(pcnt.at[0], c1, partner)
     mrow = lambda i: mext.at[pl.ds(pl.multiple_of(i * 64, 64), 64), own]
     mhalf = lambda i, h: mext.at[pl.ds(pl.multiple_of(i * 64 + h * 32, 32), 32), own]
-    st_y = [Group(mext.at[0:32, own]) for h in range(2)]
-    st_yz = [Group(mext.at[0:64, own]) for h in range(2)]
-    st_z, st_far = Group(mext.at[0:128, own]), Group(mext.at[0:128, own])
+    st_y = [Group(expo.at[0:n]) for n in (256, 320)]
+    st_yz = [Group(expo.at[0:n]) for n in (512, 640)]
+    st_z, st_far = Group(expo.at[0:1152]), Group(expo.at[0:1152])
     m_h = Group(halo.at[0])
     m_h.send(mext.at[myrows, pl.ds(128, 128)], halo.at[f, 1], dleft)
     m_h.send(mext.at[myrows, pl.ds(2048, 128)], halo.at[f, 0], dright)
@@ -141,12 +136,12 @@
     st_z.same(mrow(f), fdev(fzp), fdev(fzm))
     pool_part(1, core)
 
-    for c in emb:
-        c.wait()
+    pltpu.make_async_copy(expo.at[0:320], expo.at[0:320], lsem.at[3]).wait()
+    src_rows.wait()
     t6[...] = jnp.zeros_like(t6)
     s6[...] = jnp.zeros_like(s6)
     ta, tb, tc = split3(tgt[0:10, :])
-    sa, sb, sc = split3(src[0:10, :])
+    sa, sb, sc = split3(jnp.concatenate([src[r] for r in range(10)], axis=0))
     for k, (t, s) in enumerate([(ta, sa), (ta, sb), (tb, sa), (ta, sc), (tb, sb), (tc, sa)]):
         t6[k * 16:k * 16 + 10, :] = t
         s6[k * 16:k * 16 + 10, :] = s
@@ -167,8 +162,11 @@
         m_rs.send(s1.at[xx, yy], rs.at[k], chips[k])
         m_rc.send(s1cnt.at[pl.ds(xx * 2 + yy, 1)], rscnt.at[k], chips[k])
 
+    peak = lax.fori_loop(0, 4, score_step, jnp.zeros((8, 256), F32))
+    m_h.recv()
     st_y[1].same(mhalf(f, 1), fdev(fy))
-    peak = lax.fori_loop(0, 4, score_step, jnp.zeros((8, 256), F32))
+    st_y[1].same(halo.at[f], fdev(fy))
+    st_z.same(halo.at[f], fdev(fzp), fdev(fzm))
     peak = lax.fori_loop(4, 8, score_step, peak)
     peak = jnp.max(peak, axis=0, keepdims=True)
 
@@ -186,9 +184,8 @@
     st_z.recv()
     st_far.same(mhalf(fzm, 0), fdev(fzp))
     st_far.same(mhalf(fzp, 1), fdev(fzm))
-    m_h.recv()
-    m_hs = Group(halo.at[0:7])
-    m_hs.same(halo.at[f], *f_peers)
+    st_far.same(halo.at[fzm, 0], fdev(fzp))
+    st_far.same(halo.at[fzp, 1], fdev(fzm))
     m_rs.recv()
     m_rc.recv()
     sums, cnt = s1[x, yh].astype(F32), s1cnt[pl.ds(x * 2 + yh, 1), :]
@@ -208,6 +205,7 @@
 
     st_y[1].recv()
     st_yz[1].same(mhalf(fy, 1), fdev(fzp), fdev(fzm))
+    st_yz[1].same(halo.at[fy], fdev(fzp), fdev(fzm))
     loc[0].wait()
     for k in range(4):
         wg[k * 192:(k + 1) * 192, :] = wraw[:, k, :]
@@ -238,21 +236,22 @@
     m_ca.same(ca.at[f], *f_peers)
     st_yz[1].recv()
     st_far.same(mhalf(fi(zp, 1 - yl), 1), fdev(fzm))
+    st_far.same(halo.at[fi(zp, 1 - yl)], fdev(fzm))
     m_ca.recv()
     early = list(groups)
-    gall = (gall0, gall1, gall2)
+    gall = (gall0, gall1, gall2, gall3)
+    pieces = ((0, 64), (64, 128), (128, 160), (160, 192))
     slot = lambda g, i: gall[g].at[pl.ds(2 * i, 2)]
-    several = lambda n: [Group(gall[g].at[0:2 * n]) for g in range(3)]
+    several = lambda n: [Group(gall[g].at[0:2 * n]) for g in range(4)]
     g_x, g_p = several(7), several(8)
-    for g in range(3):
-        r = dot(wg[576 + g * 64:640 + g * 64, :], ca[...].reshape(512, 256)).astype(BF)
+    for g, (lo, hi) in enumerate(pieces):
+        r = dot(wg[576 + lo:576 + hi, :], ca[...].reshape(512, 256)).astype(BF)
         gall[g][2 * d] = r[:, :128]
         gall[g][2 * d + 1] = r[:, 128:]
         g_x[g].same(slot(g, d), *chips)
         g_p[g].same(slot(g, d), partner)
 
     st_far.recv()
-    m_hs.recv()
     for i in range(8):
         mext[i * 64:(i + 1) * 64, 0:128] = halo[i, 0]
         mext[i * 64:(i + 1) * 64, 2176:2304] = halo[i, 1]
@@ -313,28 +312,31 @@
     win = [w_in[g].astype(F32) for g in range(3)]
     wcol = [[column(win[g][i:i + 1]) for i in range(2)] for g in range(3)]
 
-    def unpool(g):
-        g_p[g].recv()
+    def unpool(p):
+        lo, hi = pieces[p]
+        rows, count, g = slice(lo, hi), hi - lo, min(p, 2)
+        part = slice(lo - 64 * g, hi - 64 * g)
+        mixed = gmix if count == 64 else gmix_half
+        g_p[p].recv()
         for s in range(16):
-            parts = []
+            tiles = []
             for t in (2 * s, 2 * s + 1):
-                lhs = jnp.concatenate([gall[g][ccols[k, t]] for k in range(2)], axis=1)
-                parts.append(gall[g][t].astype(F32) + dot(lhs, ct[t]))
-            gmix[s] = jnp.concatenate(parts, axis=1).astype(BF)
-        if g < 2:
-            swap(g + 1)
-        rows = slice(g * 64, (g + 1) * 64)
+                lhs = jnp.concatenate([gall[p][ccols[k, t]] for k in range(2)], axis=1)
+                tiles.append(gall[p][t].astype(F32) + dot(lhs, ct[t]))
+            mixed[s] = jnp.concatenate(tiles, axis=1).astype(BF)
+        if p < 3:
+            swap(p + 1)
         for n in range(8):
             cols = slice(n * 256, (n + 1) * 256)
             ecols = slice(n * 256 + 128, (n + 1) * 256 + 128)
             hi_n = cluster[:, cols] >> 8
-            r = dot(gmix[...].reshape(1024, 256), ohlo[:, cols])
-            acc = r[0:64]
+            r = dot(mixed[...].reshape(16 * count, 256), ohlo[:, cols])
+            acc = r[0:count]
             for s in range(1, 16):
-                acc = jnp.where(hi_n == s, r[s * 64:(s + 1) * 64], acc)
+                acc = jnp.where(hi_n == s, r[s * count:(s + 1) * count], acc)
             pre = acc + gsum[rows, ecols]
             xi = xin[:, cols].astype(F32)
-            terms = wcol[g][0] * xi[0:1] + wcol[g][1] * xi[1:2] + bcol[g]
+            terms = wcol[g][0][part] * xi[0:1] + wcol[g][1][part] * xi[1:2] + bcol[g][part]
             if g == 0:
                 gsum[rows, ecols] = terms + pre
                 continue
@@ -342,12 +344,12 @@
                 gsum[0:64, ecols] = jax.nn.sigmoid(gsum[0:64, ecols])
                 gsum[rows, ecols] = jax.nn.sigmoid(terms + pre)
                 continue
-            update, reset = gsum[0:64, ecols], gsum[64:128, ecols]
+            update, reset = gsum[part, ecols], gsum[64 + lo - 128:64 + hi - 128, ecols]
             cand = jnp.tanh(terms + reset * pre)
             mk = (lax.broadcasted_iota(jnp.int32, (1, 256), 1) + n * 256 < nvalid).astype(F32)
-            ms = state[:, cols].astype(F32) * mk
-            out[:, cols] = ((update * ms + (1.0 - update) * cand) * mk).astype(BF)
-            cp = pltpu.make_async_copy(out.at[:, cols], out_hbm.at[:, cols], lsem.at[23])
+            ms = state[part, cols].astype(F32) * mk
+            out[part, cols] = ((update * ms + (1.0 - update) * cand) * mk).astype(BF)
+            cp = pltpu.make_async_copy(out.at[part, cols], out_hbm.at[part, cols], lsem.at[5])
             cp.start()
 
     swap(0)
@@ -357,10 +359,11 @@
     second(15)
     unpool(1)
     unpool(2)
+    unpool(3)
 
     for m in groups[len(early):]:
         m.sent()
-    pltpu.make_async_copy(out, out_hbm, lsem.at[23]).wait()
+    pltpu.make_async_copy(out, out_hbm, lsem.at[5]).wait()
     assert len(groups) == N_MSG
 
 
@@ -381,7 +384,7 @@
             V((512, 2304), BF),
             V((8, 2, 64, 128), BF),
             V((256, 2048), BF),
-            V((64, 2048), F32),
+            V((64, 2048), BF),
             V((512, 2048), BF),
             V((2, 4, 2, 64, 256), BF),
             V((2, 8, 256), F32),
@@ -391,7 +394,7 @@
             V((8, 256), F32),
             V((7, 64, 256), BF),
             V((7, 1, 256), F32),
-            V((16, 256), F32),
+            V((10, 1, 256), F32),
             V((16, 4096), F32),
             V((96, 4096), BF),
             V((96, 256), BF),
@@ -401,8 +404,10 @@
             V((8, 64, 256), BF),
             V((32, 64, 128), BF),
             V((32, 64, 128), BF),
-            V((32, 64, 128), BF),
+            V((32, 32, 128), BF),
+            V((32, 32, 128), BF),
             V((16, 64, 256), BF),
+            V((16, 32, 256), BF),
             V((192, 2304), BF),
             V((192, 2304), BF),
             V((192, 2304), F32),
@@ -414,7 +419,7 @@
             V((32, 256, 128), BF),
             pltpu.SemaphoreType.DMA((N_MSG,)),
             pltpu.SemaphoreType.DMA((N_MSG,)),
-            pltpu.SemaphoreType.DMA((24,)),
+            pltpu.SemaphoreType.DMA((6,)),
         ],
         compiler_params=pltpu.CompilerParams(collective_id=0, has_side_effects=True),
     )(

time: 53.6 us -> 53.9 us (level)
  no operation moved by 1% of the time
where the time goes in v6:
time: 53.9 us; the launch traced here: 53.7 us
  Pallas kernels  51.4 us (95%)
  local copies, waits for them, and re-layouts  1.67 us (3%)
  between operations  0.66 us (1%)
    pallas_call x1, Pallas kernels, body(): pl.pallas_call(kernel, out_shape=jax.ShapeDtypeStruct(state.shape, BF), i...  51.4 us
    unnamed x1, local copies, waits for them, and re-layouts  1.67 us

profile of v6, /device:TPU:1, one launch (start us, length us, event | category | flops | bytes accessed | tf_op | source)
XLA Modules:
  0.0 53.7 jit_solution(8928906907490582398)
XLA Ops:
  0.7 51.4 %shard_map.136 = bf16[64,2048]{1,0:T(8,128)(2,1)} custom-call(bf16[64,2048]{1,0:T(8,128)(2,1)} %state.1, bf16[2,2048]{1,0:T(2,128)(2,1)} %xin.1, bf16[16,512,128]{2,1,0:T(8,128)(2,1)} %bitcast.10, s32[4,16]{1,0:T(4,128)} %bitcast.17, s32[1]{0:T(128)S(6)} %copy.16.valid, s32[1,2048]{1,0:T(1,128)} %bitcast.16, bf16[192,4,512]{2,1,0:T(4,128)(2,1)} %bitcast.12, ...), custom_call_target="tpu_custom_call" | custom-call | tf_op jit(solution)/shard_map/pallas_call | solution.py:378
  52.0 1.7 %copy.17 = bf16[64,2048]{1,0:T(8,128)(2,1)} copy(bf16[64,2048]{1,0:T(8,128)(2,1)} %shard_map.136) | data formatting | bytes 524288

commit v7 on v6

--- a/solution.py
+++ b/solution.py
@@ -8,7 +8,7 @@
 MESH = pl.DeviceIdType.MESH
 BF = jnp.bfloat16
 F32 = jnp.float32
-N_MSG = 25
+N_MSG = 26
 
 
 def dot(a, b, dims=((1,), (0,))):
@@ -96,26 +96,25 @@
     own = pl.ds(128, 2048)
     base[...] = masked32.astype(BF)
     mext[myrows, own] = base[...]
-    low = cluster[...] & 255
-    high = cluster[...] >> 8
-    ohlo[...] = (lax.broadcasted_iota(jnp.int32, (256, 2048), 0) == low).astype(F32).astype(BF)
-
+    low = cluster[...] & 511
+    high = cluster[...] >> 9
     row8 = lax.broadcasted_iota(jnp.int32, (8, 2048), 0)
-    row_high = (row8 & 1) * 8 + (row8 >> 1) * 2
+    cnt_lhs = jnp.where(high == (row8 & 1) * 4 + (row8 >> 1), mask, 0.0).astype(BF)
 
     def pool_part(c, to_core):
-        for xx in range(4):
-            for yy in range(2):
-                slot = xx * 2 + yy
-                hit = high == (yy * 8 + xx * 2) + to_core
-                pl_lhs[slot * 64:(slot + 1) * 64, :] = base[...] * hit.astype(F32).astype(BF)
+        rows = pl.ds(pl.multiple_of(to_core * 256, 256), 256)
+        row = lax.broadcasted_iota(jnp.int32, (256, 2048), 0) + to_core * 256
+        ohlo[rows, :] = (row == low).astype(F32).astype(BF)
         for i in range(2):
-            res = dot(pl_lhs[i * 256:(i + 1) * 256, :], ohlo[...], ((1,), (1,))).astype(BF)
+            if c == 0:
+                for slot in range(i * 4, i * 4 + 4):
+                    hit = high == (slot % 2) * 4 + slot // 2
+                    pl_lhs[slot * 64:(slot + 1) * 64, :] = base[...] * hit.astype(F32).astype(BF)
+            res = dot(pl_lhs[i * 256:(i + 1) * 256, :], ohlo[rows, :], ((1,), (1,))).astype(BF)
             for k in range(4):
                 slot = i * 4 + k
                 pool[c, slot // 2, slot % 2] = res[k * 64:(k + 1) * 64]
-        lhs = jnp.where(high == row_high + to_core, mask, 0.0).astype(BF)
-        pcnt[c] = dot(lhs, ohlo[...], ((1,), (1,)))
+        pcnt[c] = dot(cnt_lhs, ohlo[rows, :], ((1,), (1,)))
 
     pool_part(0, 1 - core)
 
@@ -231,25 +230,37 @@
     att = attend(att, mine_of(range(3, 7), 1 - core))
     swap_far.recv()
     att = attend(att, mine_of(range(3), 1 - core))
-    ca[f] = (pooled + att * inv).astype(BF)
-    m_ca = Group(ca.at[0:7])
-    m_ca.same(ca.at[f], *f_peers)
+    attn = (pooled + att * inv).astype(BF)
+    m_ca = [Group(ca.at[0, 0:7]) for h in range(2)]
+    for h in range(2):
+        ca[h, f] = attn[:, h * 128:(h + 1) * 128]
+    for h in range(2):
+        m_ca[h].same(ca.at[h, f], *f_peers)
     st_yz[1].recv()
     st_far.same(mhalf(fi(zp, 1 - yl), 1), fdev(fzm))
     st_far.same(halo.at[fi(zp, 1 - yl)], fdev(fzm))
-    m_ca.recv()
     early = list(groups)
     gall = (gall0, gall1, gall2, gall3)
     pieces = ((0, 64), (64, 128), (128, 160), (160, 192))
     slot = lambda g, i: gall[g].at[pl.ds(2 * i, 2)]
     several = lambda n: [Group(gall[g].at[0:2 * n]) for g in range(4)]
     g_x, g_p = several(7), several(8)
-    for g, (lo, hi) in enumerate(pieces):
-        r = dot(wg[576 + lo:576 + hi, :], ca[...].reshape(512, 256)).astype(BF)
-        gall[g][2 * d] = r[:, :128]
-        gall[g][2 * d + 1] = r[:, 128:]
-        g_x[g].same(slot(g, d), *chips)
-        g_p[g].same(slot(g, d), partner)
+
+    def g_send(g, h):
+        g_x[g].same(gall[g].at[2 * d + h], *chips)
+        g_p[g].same(gall[g].at[2 * d + h], partner)
+
+    for h in range(2):
+        m_ca[h].recv()
+        for g, (lo, hi) in enumerate(pieces):
+            gall[g][2 * d + h] = dot(wg[576 + lo:576 + hi, :], ca[h].reshape(512, 128)).astype(BF)
+            if g == 0 or g == 1 and h == 1:
+                g_send(g, h)
+        if h == 0:
+            g_send(1, 0)
+    for g in (2, 3):
+        for h in range(2):
+            g_send(g, h)
 
     st_far.recv()
     for i in range(8):
@@ -318,9 +329,9 @@
         part = slice(lo - 64 * g, hi - 64 * g)
         mixed = gmix if count == 64 else gmix_half
         g_p[p].recv()
-        for s in range(16):
+        for s in range(8):
             tiles = []
-            for t in (2 * s, 2 * s + 1):
+            for t in range(4 * s, 4 * s + 4):
                 lhs = jnp.concatenate([gall[p][ccols[k, t]] for k in range(2)], axis=1)
                 tiles.append(gall[p][t].astype(F32) + dot(lhs, ct[t]))
             mixed[s] = jnp.concatenate(tiles, axis=1).astype(BF)
@@ -329,10 +340,10 @@
         for n in range(8):
             cols = slice(n * 256, (n + 1) * 256)
             ecols = slice(n * 256 + 128, (n + 1) * 256 + 128)
-            hi_n = cluster[:, cols] >> 8
-            r = dot(mixed[...].reshape(16 * count, 256), ohlo[:, cols])
+            hi_n = cluster[:, cols] >> 9
+            r = dot(mixed[...].reshape(8 * count, 512), ohlo[:, cols])
             acc = r[0:count]
-            for s in range(1, 16):
+            for s in range(1, 8):
                 acc = jnp.where(hi_n == s, r[s * count:(s + 1) * count], acc)
             pre = acc + gsum[rows, ecols]
             xi = xin[:, cols].astype(F32)
@@ -383,7 +394,7 @@
         scratch_shapes=[
             V((512, 2304), BF),
             V((8, 2, 64, 128), BF),
-            V((256, 2048), BF),
+            V((512, 2048), BF),
             V((64, 2048), BF),
             V((512, 2048), BF),
             V((2, 4, 2, 64, 256), BF),
@@ -401,13 +412,13 @@
             V((4096, 256), F32),
             V((4096, 256), BF),
             V((16, 64, 256), BF),
-            V((8, 64, 256), BF),
+            V((2, 8, 64, 128), BF),
             V((32, 64, 128), BF),
             V((32, 64, 128), BF),
             V((32, 32, 128), BF),
             V((32, 32, 128), BF),
-            V((16, 64, 256), BF),
-            V((16, 32, 256), BF),
+            V((8, 64, 512), BF),
+            V((8, 32, 512), BF),
             V((192, 2304), BF),
             V((192, 2304), BF),
             V((192, 2304), F32),

time: 53.9 us -> 53.2 us (0.987)
  Pallas kernels: 51.4 us -> 50.7 us
    pallas_call x1, Pallas kernels: 51.4 us -> 50.7 us  [body(): pl.pallas_call(kernel, out_shape=jax.ShapeDtypeStruct(state.shape, BF), i...]
where the time goes in v7:
time: 53.2 us; the launch traced here: 53 us
  Pallas kernels  50.7 us (95%)
  local copies, waits for them, and re-layouts  1.67 us (3%)
  between operations  0.66 us (1%)
    pallas_call x1, Pallas kernels, body(): pl.pallas_call(kernel, out_shape=jax.ShapeDtypeStruct(state.shape, BF), i...  50.7 us
    unnamed x1, local copies, waits for them, and re-layouts  1.67 us

profile of v7, /device:TPU:1, one launch (start us, length us, event | category | flops | bytes accessed | tf_op | source)
XLA Modules:
  0.0 53.0 jit_solution(14709769005346201192)
XLA Ops:
  0.7 50.7 %shard_map.136 = bf16[64,2048]{1,0:T(8,128)(2,1)} custom-call(bf16[64,2048]{1,0:T(8,128)(2,1)} %state.1, bf16[2,2048]{1,0:T(2,128)(2,1)} %xin.1, bf16[16,512,128]{2,1,0:T(8,128)(2,1)} %bitcast.10, s32[4,16]{1,0:T(4,128)} %bitcast.17, s32[1]{0:T(128)S(6)} %copy.16.valid, s32[1,2048]{1,0:T(1,128)} %bitcast.16, bf16[192,4,512]{2,1,0:T(4,128)(2,1)} %bitcast.12, ...), custom_call_target="tpu_custom_call" | custom-call | tf_op jit(solution)/shard_map/pallas_call | solution.py:389
  51.4 1.7 %copy.17 = bf16[64,2048]{1,0:T(8,128)(2,1)} copy(bf16[64,2048]{1,0:T(8,128)(2,1)} %shard_map.136) | data formatting | bytes 524288

commit v8 on v7

--- a/solution.py
+++ b/solution.py
@@ -8,7 +8,7 @@
 MESH = pl.DeviceIdType.MESH
 BF = jnp.bfloat16
 F32 = jnp.float32
-N_MSG = 26
+N_MSG = 24
 
 
 def dot(a, b, dims=((1,), (0,))):
@@ -25,9 +25,9 @@
 
 def kernel(
     state, xin, adj_hbm, adj_cols, valid, cluster, wg_hbm, w_in, bias, w_val, src_hbm, tgt_hbm,
-    ct_hbm, ccols, out_hbm,
+    ct_hbm, ccols, out,
     mext, halo, ohlo, base, pl_lhs, pool, pcnt, r1, c1, s1, s1cnt, rs, rscnt, src, tgt, t6, s6, scores, expo,
-    vals, ca, gall0, gall1, gall2, gall3, gmix, gmix_half, ubuf, vbuf, w1m, gsum, out, adj, wraw, wg, ct,
+    vals, ca, gall0, gall1, gall2, gmix, ubuf, vbuf, w1m, gsum, adj, wraw, wg, ct,
     ssem, rsem, lsem,
 ):
     d = lax.axis_index("dom")
@@ -240,10 +240,10 @@
     st_far.same(mhalf(fi(zp, 1 - yl), 1), fdev(fzm))
     st_far.same(halo.at[fi(zp, 1 - yl)], fdev(fzm))
     early = list(groups)
-    gall = (gall0, gall1, gall2, gall3)
-    pieces = ((0, 64), (64, 128), (128, 160), (160, 192))
+    gall = (gall0, gall1, gall2)
+    pieces = ((0, 64), (64, 128), (128, 192))
     slot = lambda g, i: gall[g].at[pl.ds(2 * i, 2)]
-    several = lambda n: [Group(gall[g].at[0:2 * n]) for g in range(4)]
+    several = lambda n: [Group(gall[g].at[0:2 * n]) for g in range(3)]
     g_x, g_p = several(7), several(8)
 
     def g_send(g, h):
@@ -258,9 +258,8 @@
                 g_send(g, h)
         if h == 0:
             g_send(1, 0)
-    for g in (2, 3):
-        for h in range(2):
-            g_send(g, h)
+    for h in range(2):
+        g_send(2, h)
 
     st_far.recv()
     for i in range(8):
@@ -327,21 +326,20 @@
         lo, hi = pieces[p]
         rows, count, g = slice(lo, hi), hi - lo, min(p, 2)
         part = slice(lo - 64 * g, hi - 64 * g)
-        mixed = gmix if count == 64 else gmix_half
         g_p[p].recv()
         for s in range(8):
             tiles = []
             for t in range(4 * s, 4 * s + 4):
                 lhs = jnp.concatenate([gall[p][ccols[k, t]] for k in range(2)], axis=1)
                 tiles.append(gall[p][t].astype(F32) + dot(lhs, ct[t]))
-            mixed[s] = jnp.concatenate(tiles, axis=1).astype(BF)
-        if p < 3:
+            gmix[s] = jnp.concatenate(tiles, axis=1).astype(BF)
+        if p < 2:
             swap(p + 1)
         for n in range(8):
             cols = slice(n * 256, (n + 1) * 256)
             ecols = slice(n * 256 + 128, (n + 1) * 256 + 128)
             hi_n = cluster[:, cols] >> 9
-            r = dot(mixed[...].reshape(8 * count, 512), ohlo[:, cols])
+            r = dot(gmix[...].reshape(8 * count, 512), ohlo[:, cols])
             acc = r[0:count]
             for s in range(1, 8):
                 acc = jnp.where(hi_n == s, r[s * count:(s + 1) * count], acc)
@@ -360,8 +358,6 @@
             mk = (lax.broadcasted_iota(jnp.int32, (1, 256), 1) + n * 256 < nvalid).astype(F32)
             ms = state[part, cols].astype(F32) * mk
             out[part, cols] = ((update * ms + (1.0 - update) * cand) * mk).astype(BF)
-            cp = pltpu.make_async_copy(out.at[part, cols], out_hbm.at[part, cols], lsem.at[5])
-            cp.start()
 
     swap(0)
     unpool(0)
@@ -370,11 +366,9 @@
     second(15)
     unpool(1)
     unpool(2)
-    unpool(3)
 
     for m in groups[len(early):]:
         m.sent()
-    pltpu.make_async_copy(out, out_hbm, lsem.at[5]).wait()
     assert len(groups) == N_MSG
 
 
@@ -388,9 +382,9 @@
     V = pltpu.VMEM
     return pl.pallas_call(
         kernel,
-        out_shape=jax.ShapeDtypeStruct(state.shape, BF),
+        out_shape=pltpu.VMEM(state.shape, BF),
         in_specs=[vm, vm, hb, sm, sm, vm, hb, vm, vm, vm, hb, hb, hb, sm],
-        out_specs=hb,
+        out_specs=vm,
         scratch_shapes=[
             V((512, 2304), BF),
             V((8, 2, 64, 128), BF),
@@ -415,22 +409,19 @@
             V((2, 8, 64, 128), BF),
             V((32, 64, 128), BF),
             V((32, 64, 128), BF),
-            V((32, 32, 128), BF),
-            V((32, 32, 128), BF),
+            V((32, 64, 128), BF),
             V((8, 64, 512), BF),
-            V((8, 32, 512), BF),
             V((192, 2304), BF),
             V((192, 2304), BF),
             V((192, 2304), F32),
             V((192, 2304), F32),
-            V((64, 2048), BF),
             V((16, 512, 128), BF),
             V((192, 4, 512), BF),
             V((768, 512), BF),
             V((32, 256, 128), BF),
             pltpu.SemaphoreType.DMA((N_MSG,)),
             pltpu.SemaphoreType.DMA((N_MSG,)),
-            pltpu.SemaphoreType.DMA((6,)),
+            pltpu.SemaphoreType.DMA((5,)),
         ],
         compiler_params=pltpu.CompilerParams(collective_id=0, has_side_effects=True),
     )(

time: 53.2 us -> 50.6 us (0.951)
  Pallas kernels: 50.7 us -> 49.1 us
  local copies, waits for them, and re-layouts: 1.67 us -> 0.71 us
    pallas_call x1, Pallas kernels: 50.7 us -> 49.1 us  [body(): pl.pallas_call(kernel, out_shape=pltpu.VMEM(state.shape, BF), in_specs=[v...]
    unnamed x1, local copies, waits for them, and re-layouts: 1.67 us -> 0.71 us
where the time goes in v8:
time: 50.6 us; the launch traced here: 50.5 us
  Pallas kernels  49.1 us (97%)
  local copies, waits for them, and re-layouts  0.71 us (1%)
  between operations  0.66 us (1%)
    pallas_call x1, Pallas kernels, body(): pl.pallas_call(kernel, out_shape=pltpu.VMEM(state.shape, BF), in_specs=[v...  49.1 us

profile of v8, /device:TPU:1, one launch (start us, length us, event | category | flops | bytes accessed | tf_op | source)
XLA Modules:
  0.0 50.5 jit_solution(13205247985832812480)
XLA Ops:
  0.7 49.1 %shard_map.136 = bf16[64,2048]{1,0:T(8,128)(2,1)S(1)} custom-call(bf16[64,2048]{1,0:T(8,128)(2,1)} %state.1, bf16[2,2048]{1,0:T(2,128)(2,1)} %xin.1, bf16[16,512,128]{2,1,0:T(8,128)(2,1)} %bitcast.10, s32[4,16]{1,0:T(4,128)} %bitcast.17, s32[1]{0:T(128)S(6)} %copy.17.valid, s32[1,2048]{1,0:T(1,128)} %bitcast.16, bf16[192,4,512]{2,1,0:T(4,128)(2,1)} %bitcast.12, ...), custom_call_target="tpu_custom_call" | custom-call | tf_op jit(solution)/shard_map/pallas_call | solution.py:383
  49.8 0.7 %copy.16 = bf16[64,2048]{1,0:T(8,128)(2,1)} copy(bf16[64,2048]{1,0:T(8,128)(2,1)S(1)} %shard_map.136) | data formatting | bytes 524288

commit v9 on v8

--- a/solution.py
+++ b/solution.py
@@ -8,7 +8,7 @@
 MESH = pl.DeviceIdType.MESH
 BF = jnp.bfloat16
 F32 = jnp.float32
-N_MSG = 24
+N_MSG = 27
 
 
 def dot(a, b, dims=((1,), (0,))):
@@ -26,7 +26,7 @@
 def kernel(
     state, xin, adj_hbm, adj_cols, valid, cluster, wg_hbm, w_in, bias, w_val, src_hbm, tgt_hbm,
     ct_hbm, ccols, out,
-    mext, halo, ohlo, base, pl_lhs, pool, pcnt, r1, c1, s1, s1cnt, rs, rscnt, src, tgt, t6, s6, scores, expo,
+    mext, halo, ohlo, base, pl_lhs, pool, pcnt, r1, c1, s1, s1cnt, rs, rscnt, src, tgt, t6, s6, scores, expo, stat, stat_in, part, part_in,
     vals, ca, gall0, gall1, gall2, gmix, ubuf, vbuf, w1m, gsum, adj, wraw, wg, ct,
     ssem, rsem, lsem,
 ):
@@ -44,7 +44,9 @@
     dleft, dright = dev((d + 15) % 16), dev((d + 1) % 16)
     fi = lambda a, b: a * 2 + b
     fy, fzp, fzm = f + 1 - 2 * yl, fi(zp, yl), fi(zm, yl)
-    f_peers = [fdev((f + k) % 8) for k in range(1, 8)]
+    z2 = (z + 2) % 4
+    f_peers = [fdev(fi(*i)) for i in ((z2, 1 - yl), (z2, yl), (zp, 1 - yl), (zm, 1 - yl))]
+    f_peers += [fdev(fzp), fdev(fzm), fdev(fy)]
 
     groups = []
 
@@ -72,7 +74,7 @@
         def sent(self):
             self.copy(self.whole, self.whole, partner).wait_send()
 
-    mine = pl.ds(pl.multiple_of(d * 256, 256), 256)
+    mine = pl.ds(pl.multiple_of((yh * 4 + x) * 512, 512), 512)
     loc = [
         pltpu.make_async_copy(wg_hbm, wraw, lsem.at[0]),
         pltpu.make_async_copy(adj_hbm, adj, lsem.at[1]),
@@ -125,9 +127,9 @@
     m_c1.send(pcnt.at[0], c1, partner)
     mrow = lambda i: mext.at[pl.ds(pl.multiple_of(i * 64, 64), 64), own]
     mhalf = lambda i, h: mext.at[pl.ds(pl.multiple_of(i * 64 + h * 32, 32), 32), own]
-    st_y = [Group(expo.at[0:n]) for n in (256, 320)]
-    st_yz = [Group(expo.at[0:n]) for n in (512, 640)]
-    st_z, st_far = Group(expo.at[0:1152]), Group(expo.at[0:1152])
+    st_y = [Group(expo.at[0:n]) for n in (128, 160)]
+    st_yz = [Group(expo.at[0:n]) for n in (256, 320)]
+    st_z, st_far = Group(expo.at[0:576]), Group(expo.at[0:576])
     m_h = Group(halo.at[0])
     m_h.send(mext.at[myrows, pl.ds(128, 128)], halo.at[f, 1], dleft)
     m_h.send(mext.at[myrows, pl.ds(2048, 128)], halo.at[f, 0], dright)
@@ -135,7 +137,7 @@
     st_z.same(mrow(f), fdev(fzp), fdev(fzm))
     pool_part(1, core)
 
-    pltpu.make_async_copy(expo.at[0:320], expo.at[0:320], lsem.at[3]).wait()
+    pltpu.make_async_copy(expo.at[0:160], expo.at[0:160], lsem.at[3]).wait()
     src_rows.wait()
     t6[...] = jnp.zeros_like(t6)
     s6[...] = jnp.zeros_like(s6)
@@ -146,10 +148,10 @@
         s6[k * 16:k * 16 + 10, :] = s
 
     def score_step(j, peak):
-        cols = pl.ds(pl.multiple_of(j * 512, 512), 512)
+        cols = pl.ds(pl.multiple_of((j * 2 + core) * 256, 256), 256)
         s = jnp.maximum(dot(t6[:, cols], s6[...], ((0,), (0,))), 0.0)
-        scores[cols, :] = s
-        return jnp.maximum(peak, jnp.max(s.reshape(64, 8, 256), axis=0))
+        scores[pl.ds(pl.multiple_of(j * 256, 256), 256), :] = s
+        return jnp.maximum(peak, jnp.max(s.reshape(32, 8, 512), axis=0))
 
     m_r1.recv()
     m_c1.recv()
@@ -161,7 +163,7 @@
         m_rs.send(s1.at[xx, yy], rs.at[k], chips[k])
         m_rc.send(s1cnt.at[pl.ds(xx * 2 + yy, 1)], rscnt.at[k], chips[k])
 
-    peak = lax.fori_loop(0, 4, score_step, jnp.zeros((8, 256), F32))
+    peak = lax.fori_loop(0, 4, score_step, jnp.zeros((8, 512), F32))
     m_h.recv()
     st_y[1].same(mhalf(f, 1), fdev(fy))
     st_y[1].same(halo.at[f], fdev(fy))
@@ -170,13 +172,18 @@
     peak = jnp.max(peak, axis=0, keepdims=True)
 
     def exp_step(j, total):
-        cols = pl.ds(pl.multiple_of(j * 512, 512), 512)
-        e = jnp.exp(scores[cols, :] - peak)
-        expo[cols, :] = e.astype(BF)
-        return total + jnp.sum(e.reshape(64, 8, 256), axis=0)
-
-    total = lax.fori_loop(0, 8, exp_step, jnp.zeros((8, 256), F32))
-    inv = 1.0 / jnp.sum(total, axis=0, keepdims=True)
+        rows = pl.ds(pl.multiple_of(j * 256, 256), 256)
+        e = jnp.exp(scores[rows, :] - peak)
+        expo[rows, :] = e.astype(BF)
+        return total + jnp.sum(e.reshape(32, 8, 512), axis=0)
+
+    total = lax.fori_loop(0, 8, exp_step, jnp.zeros((8, 512), F32))
+    total = jnp.sum(total, axis=0, keepdims=True)
+    both = jnp.concatenate([peak, total], axis=0)
+    for h in range(2):
+        stat[h] = both[:, h * 256:(h + 1) * 256]
+    m_stat = Group(stat_in)
+    m_stat.send(stat.at[1 - core], stat_in, partner)
 
     st_y[0].recv()
     st_yz[0].same(mhalf(fy, 0), fdev(fzp), fdev(fzm))
@@ -199,9 +206,6 @@
     near, far = Group(vals.at[0:4]), Group(vals.at[0:3])
     for k in range(7):
         (far if k < 3 else near).same(vals.at[d], chips[k])
-    swap_near, swap_far = Group(vals.at[0:5]), Group(vals.at[0:3])
-    swap_near.same(vals.at[d], partner)
-
     st_y[1].recv()
     st_yz[1].same(mhalf(fy, 1), fdev(fzp), fdev(fzm))
     st_yz[1].same(halo.at[fy], fdev(fzp), fdev(fzm))
@@ -209,28 +213,31 @@
     for k in range(4):
         wg[k * 192:(k + 1) * 192, :] = wraw[:, k, :]
 
-    def attend(total, slots):
-        for i in slots:
-            rows = pl.ds(pl.multiple_of(i * 256, 256), 256)
-            total = total + dot(vals[i], expo[rows, :])
+    def attend(total, chips_at):
+        for i in chips_at:
+            rows = pl.ds(pl.multiple_of(i * 128, 256), 256)
+            total = total + dot(vals[i + core], expo[rows, :])
         return total
 
     st_yz[0].recv()
     st_far.same(mhalf(fi(zm, 1 - yl), 0), fdev(fzp))
     mine_of = lambda ks, c: [chip(*hops[k]) + c for k in ks]
+    at = lambda ks: [chip(*hops[k]) for k in ks]
     near.recv()
-    for i in mine_of(range(3, 7), core):
-        swap_near.same(vals.at[i], partner)
-    att = attend(jnp.zeros((64, 256), F32), [d] + mine_of(range(3, 7), core))
+    att = attend(jnp.zeros((64, 512), F32), [chip(0, 0)] + at(range(3, 7)))
     far.recv()
-    for i in mine_of(range(3), core):
-        swap_far.same(vals.at[i], partner)
-    swap_near.recv()
-    att = attend(att, mine_of(range(3), core) + [chip(0, 0) + 1 - core])
-    att = attend(att, mine_of(range(3, 7), 1 - core))
-    swap_far.recv()
-    att = attend(att, mine_of(range(3), 1 - core))
-    attn = (pooled + att * inv).astype(BF)
+    att = attend(att, at(range(3)))
+    for h in range(2):
+        part[h] = att[:, h * 256:(h + 1) * 256]
+    m_part = Group(part_in)
+    m_part.send(part.at[1 - core], part_in, partner)
+    m_stat.recv()
+    peaks = stat[core, 0:1, :], stat_in[0:1, :]
+    top = jnp.maximum(*peaks)
+    wa, wb = (jnp.exp(i - top) for i in peaks)
+    inv = 1.0 / (stat[core, 1:2, :] * wa + stat_in[1:2, :] * wb)
+    m_part.recv()
+    attn = (pooled + part[core] * (wa * inv) + part_in[...] * (wb * inv)).astype(BF)
     m_ca = [Group(ca.at[0, 0:7]) for h in range(2)]
     for h in range(2):
         ca[h, f] = attn[:, h * 128:(h + 1) * 128]
@@ -244,10 +251,11 @@
     pieces = ((0, 64), (64, 128), (128, 192))
     slot = lambda g, i: gall[g].at[pl.ds(2 * i, 2)]
     several = lambda n: [Group(gall[g].at[0:2 * n]) for g in range(3)]
-    g_x, g_p = several(7), several(8)
+    g_far, g_near, g_p = several(3), several(4), several(8)
 
     def g_send(g, h):
-        g_x[g].same(gall[g].at[2 * d + h], *chips)
+        g_far[g].same(gall[g].at[2 * d + h], *chips[:3])
+        g_near[g].same(gall[g].at[2 * d + h], *chips[3:])
         g_p[g].same(gall[g].at[2 * d + h], partner)
 
     for h in range(2):
@@ -307,9 +315,10 @@
     for t in range(1, 15):
         second(t)
     def swap(g):
-        g_x[g].recv()
-        for i in mine_of(range(7), core):
-            g_p[g].same(slot(g, i), partner)
+        for group, ks in ((g_near, range(3, 7)), (g_far, range(3))):
+            group[g].recv()
+            for i in mine_of(ks, core):
+                g_p[g].same(slot(g, i), partner)
 
     for m in early:
         m.sent()
@@ -399,12 +408,16 @@
             V((8, 256), F32),
             V((7, 64, 256), BF),
             V((7, 1, 256), F32),
-            V((10, 1, 256), F32),
+            V((10, 1, 512), F32),
             V((16, 4096), F32),
             V((96, 4096), BF),
-            V((96, 256), BF),
-            V((4096, 256), F32),
-            V((4096, 256), BF),
+            V((96, 512), BF),
+            V((2048, 512), F32),
+            V((2048, 512), BF),
+            V((2, 2, 256), F32),
+            V((2, 256), F32),
+            V((2, 64, 256), F32),
+            V((64, 256), F32),
             V((16, 64, 256), BF),
             V((2, 8, 64, 128), BF),
             V((32, 64, 128), BF),

time: 50.6 us -> 50.6 us (level)
  no operation moved by 1% of the time
where the time goes in v9:
time: 50.6 us; the launch traced here: 50.5 us
  Pallas kernels  49.1 us (97%)
  local copies, waits for them, and re-layouts  0.71 us (1%)
  between operations  0.66 us (1%)
    pallas_call x1, Pallas kernels, body(): pl.pallas_call(kernel, out_shape=pltpu.VMEM(state.shape, BF), in_specs=[v...  49.1 us

profile of v9, /device:TPU:1, one launch (start us, length us, event | category | flops | bytes accessed | tf_op | source)
XLA Modules:
  0.0 50.5 jit_solution(14454642133357062779)
XLA Ops:
  0.7 49.1 %shard_map.136 = bf16[64,2048]{1,0:T(8,128)(2,1)S(1)} custom-call(bf16[64,2048]{1,0:T(8,128)(2,1)} %state.1, bf16[2,2048]{1,0:T(2,128)(2,1)} %xin.1, bf16[16,512,128]{2,1,0:T(8,128)(2,1)} %bitcast.10, s32[4,16]{1,0:T(4,128)} %bitcast.17, s32[1]{0:T(128)S(6)} %copy.17.valid, s32[1,2048]{1,0:T(1,128)} %bitcast.16, bf16[192,4,512]{2,1,0:T(4,128)(2,1)} %bitcast.12, ...), custom_call_target="tpu_custom_call" | custom-call | tf_op jit(solution)/shard_map/pallas_call | solution.py:392
  49.8 0.7 %copy.16 = bf16[64,2048]{1,0:T(8,128)(2,1)} copy(bf16[64,2048]{1,0:T(8,128)(2,1)S(1)} %shard_map.136) | data formatting | bytes 524288

commit v10 on v9

--- a/solution.py
+++ b/solution.py
@@ -219,8 +219,6 @@
             total = total + dot(vals[i + core], expo[rows, :])
         return total
 
-    st_yz[0].recv()
-    st_far.same(mhalf(fi(zm, 1 - yl), 0), fdev(fzp))
     mine_of = lambda ks, c: [chip(*hops[k]) + c for k in ks]
     at = lambda ks: [chip(*hops[k]) for k in ks]
     near.recv()
@@ -243,6 +241,8 @@
         ca[h, f] = attn[:, h * 128:(h + 1) * 128]
     for h in range(2):
         m_ca[h].same(ca.at[h, f], *f_peers)
+    st_yz[0].recv()
+    st_far.same(mhalf(fi(zm, 1 - yl), 0), fdev(fzp))
     st_yz[1].recv()
     st_far.same(mhalf(fi(zp, 1 - yl), 1), fdev(fzm))
     st_far.same(halo.at[fi(zp, 1 - yl)], fdev(fzm))

time: 50.6 us -> 49.1 us (0.970)
  Pallas kernels: 49.1 us -> 47.6 us
    pallas_call x1, Pallas kernels: 49.1 us -> 47.6 us  [body(): pl.pallas_call(kernel, out_shape=pltpu.VMEM(state.shape, BF), in_specs=[v...]
where the time goes in v10:
time: 49.1 us; the launch traced here: 48.9 us
  Pallas kernels  47.6 us (97%)
  local copies, waits for them, and re-layouts  0.71 us (1%)
  between operations  0.66 us (1%)
    pallas_call x1, Pallas kernels, body(): pl.pallas_call(kernel, out_shape=pltpu.VMEM(state.shape, BF), in_specs=[v...  47.6 us

profile of v10, /device:TPU:1, one launch (start us, length us, event | category | flops | bytes accessed | tf_op | source)
XLA Modules:
  0.0 48.9 jit_solution(9909382160995343352)
XLA Ops:
  0.7 47.6 %shard_map.136 = bf16[64,2048]{1,0:T(8,128)(2,1)S(1)} custom-call(bf16[64,2048]{1,0:T(8,128)(2,1)} %state.1, bf16[2,2048]{1,0:T(2,128)(2,1)} %xin.1, bf16[16,512,128]{2,1,0:T(8,128)(2,1)} %bitcast.10, s32[4,16]{1,0:T(4,128)} %bitcast.17, s32[1]{0:T(128)S(6)} %copy.17.valid, s32[1,2048]{1,0:T(1,128)} %bitcast.16, bf16[192,4,512]{2,1,0:T(4,128)(2,1)} %bitcast.12, ...), custom_call_target="tpu_custom_call" | custom-call | tf_op jit(solution)/shard_map/pallas_call | solution.py:392
  48.2 0.7 %copy.16 = bf16[64,2048]{1,0:T(8,128)(2,1)} copy(bf16[64,2048]{1,0:T(8,128)(2,1)S(1)} %shard_map.136) | data formatting | bytes 524288

commit v11 on v10

--- a/solution.py
+++ b/solution.py
@@ -87,7 +87,7 @@
 
     barrier = pltpu.get_barrier_semaphore()
     cross = dev((d + 15 + 2 * core) % 16)
-    peers = [partner, cross] + chips + f_peers
+    peers = chips + f_peers + [cross, partner]
     for p in peers:
         pl.semaphore_signal(barrier, inc=1, device_id=p, device_id_type=MESH)
 
@@ -262,12 +262,11 @@
         m_ca[h].recv()
         for g, (lo, hi) in enumerate(pieces):
             gall[g][2 * d + h] = dot(wg[576 + lo:576 + hi, :], ca[h].reshape(512, 128)).astype(BF)
-            if g == 0 or g == 1 and h == 1:
+            if g == 0:
                 g_send(g, h)
-        if h == 0:
-            g_send(1, 0)
-    for h in range(2):
-        g_send(2, h)
+    for g in (1, 2):
+        for h in range(2):
+            g_send(g, h)
 
     st_far.recv()
     for i in range(8):
@@ -312,14 +311,15 @@
     m_vh.send(tile(16), tile(0), dright)
     for t in range(1, 15):
         first(t)
-    for t in range(1, 15):
-        second(t)
     def swap(g):
         for group, ks in ((g_near, range(3, 7)), (g_far, range(3))):
             group[g].recv()
             for i in mine_of(ks, core):
                 g_p[g].same(slot(g, i), partner)
 
+    swap(0)
+    for t in range(1, 15):
+        second(t)
     for m in early:
         m.sent()
     loc[2].wait()
@@ -368,7 +368,6 @@
             ms = state[part, cols].astype(F32) * mk
             out[part, cols] = ((update * ms + (1.0 - update) * cand) * mk).astype(BF)
 
-    swap(0)
     unpool(0)
     m_vh.recv()
     second(0)

time: 49.1 us -> 49.1 us (level)
  no operation moved by 1% of the time
where the time goes in v11:
time: 49.1 us; the launch traced here: 49 us
  Pallas kernels  47.6 us (97%)
  local copies, waits for them, and re-layouts  0.71 us (1%)
  between operations  0.66 us (1%)
    pallas_call x1, Pallas kernels, body(): pl.pallas_call(kernel, out_shape=pltpu.VMEM(state.shape, BF), in_specs=[v...  47.6 us

profile of v11, /device:TPU:1, one launch (start us, length us, event | category | flops | bytes accessed | tf_op | source)
XLA Modules:
  0.0 49.0 jit_solution(15719416845404024820)
XLA Ops:
  0.7 47.6 %shard_map.136 = bf16[64,2048]{1,0:T(8,128)(2,1)S(1)} custom-call(bf16[64,2048]{1,0:T(8,128)(2,1)} %state.1, bf16[2,2048]{1,0:T(2,128)(2,1)} %xin.1, bf16[16,512,128]{2,1,0:T(8,128)(2,1)} %bitcast.10, s32[4,16]{1,0:T(4,128)} %bitcast.17, s32[1]{0:T(128)S(6)} %copy.17.valid, s32[1,2048]{1,0:T(1,128)} %bitcast.16, bf16[192,4,512]{2,1,0:T(4,128)(2,1)} %bitcast.12, ...), custom_call_target="tpu_custom_call" | custom-call | tf_op jit(solution)/shard_map/pallas_call | solution.py:391
  48.3 0.7 %copy.16 = bf16[64,2048]{1,0:T(8,128)(2,1)} copy(bf16[64,2048]{1,0:T(8,128)(2,1)S(1)} %shard_map.136) | data formatting | bytes 524288
